TPU v7x, 32 devices: a whole 2x2x4 slice. The times are simulated.
32 devices in a mesh: rep: 2 (over core), shard: 16 (over z, y, x).
Axes of the slice: x: 2, y: 2, z: 4, core: 2. Of those that a mesh axis runs over, the one named last changes fastest.
Arguments:
- z_state: float32 [8192, 128], P('shard'), may hold values from -12 to 12
- n_state: float32 [8192, 128], P('shard'), may hold values from 0.1 to 10
- tile_values: bfloat16 [8192, 128, 128], P(('rep', 'shard')), may hold values from -0.29882812 to 0.29882812
- tile_block: int32 [8192], P(('rep', 'shard')), may hold values from 0 to 8191, as said below
- tile_group: int32 [8192], P(('rep', 'shard')), may hold values from 0 to 7, as said below
- labels: int32 [256, 128], P(('rep', 'shard')), may hold values 0 or 1
Outputs:
- margins: float32 [256, 128], P(('rep', 'shard'))
- new_z: float32 [8192, 128], P('shard', 'rep')
- new_n: float32 [8192, 128], P('shard', 'rep')
- new_w: float32 [8192, 128], P('shard', 'rep')
Inputs may be any that keep to these rules, and one draw needn't show every extreme that they name: `tile_block`: block b belongs to server shard b // 512. Among the 256 tiles of one device, at most 18 belong to one server shard; in every draw one server shard gets exactly 18 tiles from every device. `tile_group`: each row group of a device is named by exactly 32 of its tiles.
All inputs are finite; a program needn't handle non-finite values. No bound on the sum of `labels` on one device may be relied on, other than what follows from the above.
Results may differ from a plain program's by a relative error of at most 0.0049.
Values may be sent and summed in bfloat16 or wider, within the bound.
No kernel may reach another device: no remote copies, remote signals or barrier semaphores. Data moves between devices by JAX's collectives and lax.ppermute only.
A program may use at most 64 MiB of HBM per device.

v0:
```python
import jax
import jax.numpy as jnp
from jax import lax
from jax.sharding import PartitionSpec as P

rate_alpha = 0.5
rate_beta = 1.0
lasso_weight = 0.5
ridge_weight = 1.0


def passed_along(x, axis, by):
    size = lax.axis_size(axis)
    pairs = [(i, i + by) for i in range(size) if 0 <= i + by < size]
    return lax.ppermute(x, axis, pairs)


def from_root(value, axis, source):
    kept = jnp.where(lax.axis_index(axis) == source, value, 0).astype(value.dtype)
    return lax.psum(kept, axis)


def shrink(z_acc, n_acc):
    soft = z_acc - jnp.clip(z_acc, -lasso_weight, lasso_weight)
    return -soft / ((rate_beta + jnp.sqrt(n_acc)) / rate_alpha + ridge_weight)


def update(z_state, n_state, w_old, total):
    sigma = (jnp.sqrt(n_state + total * total) - jnp.sqrt(n_state)) / rate_alpha
    new_z = z_state + total - sigma * w_old
    new_n = n_state + total * total
    return (new_z, new_n, shrink(new_z, new_n))


def body(z_state, n_state, tile_values, tile_block, tile_group, labels):
    blk_dev, lane = z_state.shape
    tiles = tile_block.shape[0]
    groups = labels.shape[0]
    shards = lax.axis_size("shard")
    cap = max(4, (tiles + shards - 2) // (shards - 1))
    w_old = shrink(z_state, n_state)
    w_pull = w_old.astype(jnp.bfloat16)
    owner = tile_block // blk_dev
    local = tile_block - owner * blk_dev
    order = jnp.arange(tiles, dtype=jnp.int32)
    earlier = (owner[None, :] == owner[:, None]) & (order[None, :] < order[:, None])
    rank = jnp.sum(earlier.astype(jnp.int32), axis=1)
    slot = owner * cap + rank
    send_ids = jnp.full((shards * cap,), -1, jnp.int32).at[slot].set(local).reshape(shards, cap)
    asked = lax.all_to_all(send_ids, "shard", split_axis=0, concat_axis=0, tiled=True)
    valid = asked >= 0
    rows = jnp.where(valid[..., None], w_pull[jnp.maximum(asked, 0)], jnp.zeros((), jnp.bfloat16))
    answer = lax.all_to_all(rows, "shard", split_axis=0, concat_axis=0, tiled=True)
    answer, asked = (answer, asked)
    pulled = answer.reshape(shards * cap, lane)[slot]
    contrib = jnp.einsum("tef,tf->te", tile_values, pulled, preferred_element_type=jnp.float32)
    member = (tile_group[None, :] == jnp.arange(groups, dtype=jnp.int32)[:, None]).astype(
        jnp.float32
    )
    margins = jnp.dot(member, contrib, precision=lax.Precision.HIGHEST)
    resid = (jax.nn.sigmoid(margins) - labels.astype(jnp.float32)).astype(jnp.bfloat16)
    per_tile = resid[tile_group]
    grads = jnp.einsum("tef,te->tf", tile_values, per_tile, preferred_element_type=jnp.float32)
    outgoing = (
        jnp.zeros((shards * cap, lane), jnp.float32).at[slot].set(grads).reshape(shards, cap, lane)
    )
    incoming = lax.all_to_all(
        outgoing.astype(jnp.bfloat16), "shard", split_axis=0, concat_axis=0, tiled=True
    ).astype(outgoing.dtype)
    valid = (asked >= 0).reshape(-1)
    partial_value = (
        jnp.zeros((blk_dev, lane), jnp.float32)
        .at[jnp.maximum(asked, 0).reshape(-1)]
        .add(jnp.where(valid[:, None], incoming.reshape(-1, lane), 0.0))
    )
    other = passed_along(partial_value.astype(jnp.bfloat16), "rep", -1).astype(partial_value.dtype)
    new_z, new_n, new_w = update(z_state, n_state, w_old, partial_value + other)
    stacked = from_root(jnp.stack([new_z, new_n, new_w]), "rep", 0)
    new_z, new_n, new_w = (stacked[0], stacked[1], stacked[2])
    half = lane // lax.axis_size("rep")
    start = lax.axis_index("rep") * half
    new_z = lax.dynamic_slice_in_dim(new_z, start, half, 1)
    new_n = lax.dynamic_slice_in_dim(new_n, start, half, 1)
    new_w = lax.dynamic_slice_in_dim(new_w, start, half, 1)
    return (margins, new_z, new_n, new_w)


def solution(mesh):
    placed = (
        P("shard", None),
        P("shard", None),
        P(("rep", "shard"), None, None),
        P(("rep", "shard")),
        P(("rep", "shard")),
        P(("rep", "shard"), None),
    )
    return jax.shard_map(
        body,
        mesh=mesh,
        in_specs=placed,
        out_specs=(
            P(("rep", "shard"), None),
            P("shard", "rep"),
            P("shard", "rep"),
            P("shard", "rep"),
        ),
        check_vma=False,
    )
```

profile of v0, /device:TPU:0, one launch (start us, length us, event | category | flops | bytes accessed | tf_op | source)
XLA Modules:
  0.0 102.3 jit_solution(16322869634636989532)
XLA Ops:
  7.2 0.0 copy-start.2
  7.2 0.0 copy-start.3
  7.2 0.7 multiply_subtract_fusion.1
  7.9 0.2 convert_reduce_fusion
  8.1 0.7 compare_select_fusion
  8.8 1.4 %scatter_custom_fusion = s32[288]{0:T(512)S(1)} fusion(s32[256]{0:T(256)S(1)} %get-tuple-element.15, s32[256]{0:T(256)S(1)} %get-tuple-element.4, s32[]{:T(128)} %constant.19.clone.1), kind=kCustom, calls=%fused_computation.50 | custom fusion | bytes 1156 | tf_op jit(solution)/shard_map/scatter | solution.py:49
  10.2 0.7 all_to_all.12
  10.9 8.3 %all-to-all-start = ((s32[16,1,18]{2,1,0:T(1,128)}), s32[16,1,18]{2,1,0:T(1,128)S(1)}, u32[]{:S(2)}, u32[]{:S(2)}) async-start(s32[16,1,18]{2,1,0:T(1,128)} %all_to_all.12), calls=%async_computation | async-start | bytes 16384 | tf_op jit(solution)/shard_map/all_to_all | solution.py:50
  19.2 1.2 %fusion.13 = bf16[512,128]{1,0:T(8,128)(2,1)S(1)} fusion(f32[512,128]{1,0:T(8,128)} %param.7, f32[512,128]{1,0:T(8,128)} %param.6), kind=kLoop, calls=%fused_computation.27 | loop fusion | flops 524288 | bytes 655360 | tf_op jit(solution)/shard_map/convert_element_type | solution.py:42
  20.4 6.0 %all-to-all-done = s32[16,1,18]{2,1,0:T(1,128)S(1)} async-done(((s32[16,1,18]{2,1,0:T(1,128)}), s32[16,1,18]{2,1,0:T(1,128)S(1)}, u32[]{:S(2)}, u32[]{:S(2)}) %all-to-all-start) | async-done | bytes 1184 | tf_op jit(solution)/shard_map/all_to_all | solution.py:50
  26.4 0.1 reshape.76
  26.5 1.4 %gather_fusion = bf16[288,128]{1,0:T(8,128)(2,1)S(1)} fusion(bf16[512,128]{1,0:T(8,128)(2,1)S(1)} %fusion.13, s32[1024]{0:T(1024)S(1)} %pad_clamp_fusion.2), kind=kCustom, calls=%fused_computation | custom fusion | bytes 148608 | tf_op jit(solution)/shard_map/gather | solution.py:52
  27.9 0.8 broadcast_select_fusion
  28.7 3.5 %all-to-all-start.1 = ((bf16[16,18,128]{2,1,0:T(8,128)(2,1)}), bf16[16,18,128]{2,1,0:T(8,128)(2,1)S(1)}, u32[]{:S(2)}, u32[]{:S(2)}) async-start(bf16[16,18,128]{2,1,0:T(8,128)(2,1)} %broadcast_select_fusion), calls=%async_computation.1 | async-start | bytes 196608 | tf_op jit(solution)/shard_map/all_to_all | solution.py:53
  32.2 7.6 %all-to-all-done.1 = bf16[16,18,128]{2,1,0:T(8,128)(2,1)S(1)} async-done(((bf16[16,18,128]{2,1,0:T(8,128)(2,1)}), bf16[16,18,128]{2,1,0:T(8,128)(2,1)S(1)}, u32[]{:S(2)}, u32[]{:S(2)}) %all-to-all-start.1) | async-done | bytes 73760 | tf_op jit(solution)/shard_map/all_to_all | solution.py:53
  39.9 0.9 gather_fusion.1
  40.7 0.0 copy-start
  40.7 0.0 copy-start.1
  40.7 7.8 %fusion.10 = f32[256,1,128]{2,1,0:T(1,128)S(1)} fusion(bf16[256,128,128]{2,1,0:T(8,128)(2,1)} %param.8, bf16[256,128,1]{1,0,2:T(8,128)(2,1)S(1)} %bitcast.28), kind=kOutput, calls=%fused_computation.24 | convolution fusion | flops 8388608 | bytes 8585216 | tf_op jit(solution)/shard_map/tef,tf->te/dot_general | solution.py:56
  48.6 0.0 copy-done.2
  48.6 0.0 copy-done.3
  48.6 0.8 subtract_convert_fusion
  49.4 0.9 gather_fusion.2
  50.2 5.6 %fusion.8 = f32[256,1,128]{2,1,0:T(1,128)S(1)} fusion(bf16[256,128,128]{2,1,0:T(8,128)(2,1)} %param.8, bf16[256,128,1]{1,0,2:T(8,128)(2,1)S(1)} %bitcast.29), kind=kOutput, calls=%fused_computation.22 | convolution fusion | flops 8388608 | bytes 8585216 | tf_op jit(solution)/shard_map/tef,te->tf/dot_general | solution.py:63
  55.9 1.2 %scatter_custom_fusion.1 = f32[288,128]{1,0:T(8,128)S(1)} fusion(s32[256]{0:T(256)S(1)} %get-tuple-element.15, f32[256,128]{1,0:T(8,128)S(1)} %bitcast.31, f32[]{:T(128)} %constant.61.clone.1), kind=kCustom, calls=%fused_computation.31 | custom fusion | bytes 147460 | tf_op jit(solution)/shard_map/scatter | solution.py:65
  57.1 0.7 convert_element_type.33
  57.7 3.5 %all-to-all-start.2 = ((bf16[16,18,128]{2,1,0:T(8,128)(2,1)}), bf16[16,18,128]{2,1,0:T(8,128)(2,1)S(1)}, u32[]{:S(2)}, u32[]{:S(2)}) async-start(bf16[16,18,128]{2,1,0:T(8,128)(2,1)} %convert_element_type.33), calls=%async_computation.2 | async-start | bytes 196608 | tf_op jit(solution)/shard_map/all_to_all | solution.py:67
  61.3 0.0 all-reduce.2.cloned.1.call-start
  61.3 0.1 ge.20
  61.4 7.5 %all-to-all-done.2 = bf16[16,18,128]{2,1,0:T(8,128)(2,1)S(1)} async-done(((bf16[16,18,128]{2,1,0:T(8,128)(2,1)}), bf16[16,18,128]{2,1,0:T(8,128)(2,1)S(1)}, u32[]{:S(2)}, u32[]{:S(2)}) %all-to-all-start.2) | async-done | bytes 73760 | tf_op jit(solution)/shard_map/all_to_all | solution.py:67
  68.9 1.7 %scatter_custom_fusion.2 = f32[512,128]{1,0:T(8,128)S(1)} fusion(s32[288]{0:T(512)S(1)} %reshape.76, f32[288,128]{1,0:T(8,128)S(1)} %reshape.73, f32[]{:T(128)} %constant.61.clone.1, pred[288]{0:T(512)(128)(4,1)S(1)} %ge.20), kind=kCustom, calls=%fused_computation.20 | custom fusion | flops 73728 | bytes 411136 | tf_op jit(solution)/shard_map/scatter-add | solution.py:74
  70.7 1.3 %collective-permute-start = (bf16[512,128]{1,0:T(8,128)(2,1)S(1)}, bf16[512,128]{1,0:T(8,128)(2,1)S(1)}, u32[]{:S(2)}, u32[]{:S(2)}) collective-permute-start(bf16[512,128]{1,0:T(8,128)(2,1)S(1)} %convert_element_type.34), channel_id=1, source_target_pairs={{16,0},{17,1},{18,2},{19,3},{20,4},{21,5},{22,6},{23,7},{24,8},{25... | collective-permute-start | bytes 393224 | tf_op jit(solution)/shard_map/ppermute | solution.py:15
  72.0 1.9 %collective-permute-done = bf16[512,128]{1,0:T(8,128)(2,1)S(1)} collective-permute-done((bf16[512,128]{1,0:T(8,128)(2,1)S(1)}, bf16[512,128]{1,0:T(8,128)(2,1)S(1)}, u32[]{:S(2)}, u32[]{:S(2)}) %collective-permute-start) | collective-permute-done | bytes 131104 | tf_op jit(solution)/shard_map/ppermute | solution.py:15
  73.9 0.0 copy-done
  73.9 0.0 copy-done.1
  73.9 0.3 fusion.23
  74.2 0.9 maximum_select_fusion
  75.2 0.0 all-reduce.2.cloned.1.call-update
  75.2 16.3 %all-reduce.2.cloned.1.call-done = f32[3,512,128]{2,1,0:T(8,128)} async-done(((f32[3,512,128]{2,1,0:T(8,128)}), f32[3,512,128]{2,1,0:T(8,128)}) %all-reduce.2.cloned.1.call-update) | async-done | bytes 786448 | tf_op jit(solution)/shard_map/psum | solution.py:20
  91.5 1.2 %fusion.24 = (f32[1,512,128]{2,1,0:T(8,128)S(1)}, f32[1,512,128]{2,1,0:T(8,128)S(1)}, f32[1,512,128]{2,1,0:T(8,128)S(1)}) fusion(f32[3,512,128]{2,1,0:T(8,128)} %all-reduce.2.cloned.1.call-done), kind=kLoop, calls=%fused_computation.56 | loop fusion | bytes 1572864 | tf_op jit(solution)/shard_map/slice | solution.py:79
  92.7 0.1 constant_dynamic-slice_fusion
  92.8 0.8 copy.25
  93.6 0.1 constant_dynamic-slice_fusion.1
  93.7 0.8 copy.24
  94.5 0.1 constant_dynamic-slice_fusion.2
  94.7 0.8 copy.23
  (11 shorter events, 0.1 us)
Async XLA Ops:
  7.2 41.4 %copy-start.2 = (s32[256]{0:T(256)S(1)}, s32[256]{0:T(256)}, u32[]{:S(2)}) copy-start(s32[256]{0:T(256)} %param.10) | copy-start | bytes 3076
  7.2 41.4 %copy-start.3 = (s32[8,128]{1,0:T(8,128)S(1)}, s32[8,128]{1,0:T(8,128)}, u32[]{:S(2)}) copy-start(s32[8,128]{1,0:T(8,128)} %param.11) | copy-start | bytes 12292
  10.9 15.5 %all-to-all-start = ((s32[16,1,18]{2,1,0:T(1,128)}), s32[16,1,18]{2,1,0:T(1,128)S(1)}, u32[]{:S(2)}, u32[]{:S(2)}) async-start(s32[16,1,18]{2,1,0:T(1,128)} %all_to_all.12), calls=%async_computation | async-start | bytes 16384 | tf_op jit(solution)/shard_map/all_to_all | solution.py:50
  28.7 11.1 %all-to-all-start.1 = ((bf16[16,18,128]{2,1,0:T(8,128)(2,1)}), bf16[16,18,128]{2,1,0:T(8,128)(2,1)S(1)}, u32[]{:S(2)}, u32[]{:S(2)}) async-start(bf16[16,18,128]{2,1,0:T(8,128)(2,1)} %broadcast_select_fusion), calls=%async_computation.1 | async-start | bytes 196608 | tf_op jit(solution)/shard_map/all_to_all | solution.py:53
  40.7 33.2 %copy-start = (f32[512,128]{1,0:T(8,128)S(1)}, f32[512,128]{1,0:T(8,128)}, u32[]{:S(2)}) copy-start(f32[512,128]{1,0:T(8,128)} %param.7) | copy-start | bytes 786436
  40.7 33.2 %copy-start.1 = (f32[512,128]{1,0:T(8,128)S(1)}, f32[512,128]{1,0:T(8,128)}, u32[]{:S(2)}) copy-start(f32[512,128]{1,0:T(8,128)} %param.6) | copy-start | bytes 786436
  57.7 11.1 %all-to-all-start.2 = ((bf16[16,18,128]{2,1,0:T(8,128)(2,1)}), bf16[16,18,128]{2,1,0:T(8,128)(2,1)S(1)}, u32[]{:S(2)}, u32[]{:S(2)}) async-start(bf16[16,18,128]{2,1,0:T(8,128)(2,1)} %convert_element_type.33), calls=%async_computation.2 | async-start | bytes 196608 | tf_op jit(solution)/shard_map/all_to_all | solution.py:67
  61.3 30.3 %all-reduce.2.cloned.1.call-start = ((), (), s32[]{:S(2)}) async-start(), calls=%async_computation.3 | async-start | bytes 1572864 | tf_op jit(solution)/shard_map/psum | solution.py:20
  70.7 3.2 %collective-permute-start = (bf16[512,128]{1,0:T(8,128)(2,1)S(1)}, bf16[512,128]{1,0:T(8,128)(2,1)S(1)}, u32[]{:S(2)}, u32[]{:S(2)}) collective-permute-start(bf16[512,128]{1,0:T(8,128)(2,1)S(1)} %convert_element_type.34), channel_id=1, source_target_pairs={{16,0},{17,1},{18,2},{19,3},{20,4},{21,5},{22,6},{23,7},{24,8},{25... | collective-permute-start | bytes 393224 | tf_op jit(solution)/shard_map/ppermute | solution.py:15
Sparse Core Ops, SparseCore 0:
  75.3 16.1 all-reduce.1
where the time goes:
time: 103 us; the launch traced here: 102 us
  waiting for transfers between devices  39.4 us (38%)
  starting transfers between devices  16.7 us (16%)
  matrix products  14.3 us (14%)
  between operations  14.2 us (14%)
  local copies, waits for them, and re-layouts  11.2 us (11%)
  other arithmetic  6.56 us (6%)
    psum x1, waiting for transfers between devices, from_root(): return lax.psum(kept, axis)  16.3 us
    all_to_all x1, starting transfers between devices, body(): lax.all_to_all(send_ids, 'shard', split_axis=0, concat_axis=0, tiled=True)  8.31 us
    dot_general x1, matrix products, body(): jnp.einsum('tef,tf->te', tile_values, pulled, preferred_element_type=jnp....  7.83 us
    all_to_all x1, waiting for transfers between devices, body(): lax.all_to_all(rows, 'shard', split_axis=0, concat_axis=0, tiled=True)  7.61 us
    all_to_all x1, waiting for transfers between devices, body(): lax.all_to_all(outgoing.astype(jnp.bfloat16), 'shard', split_axis=0, conc...  7.48 us
    all_to_all x1, waiting for transfers between devices, body(): lax.all_to_all(send_ids, 'shard', split_axis=0, concat_axis=0, tiled=True)  6.02 us
    dot_general x1, matrix products, body(): jnp.einsum('tef,te->tf', tile_values, per_tile, preferred_element_type=jn...  5.65 us
    all_to_all x1, starting transfers between devices, body(): lax.all_to_all(rows, 'shard', split_axis=0, concat_axis=0, tiled=True)  3.51 us
  transfers between devices with their start and end apart: 5, of which 5 were waited for; matrix products, arithmetic and copies ran while one was open for 1% of the time, Pallas kernels for 0%

commit v1 on v0

v1 whole, which is shorter than its diff:
```python
import functools

import jax
import jax.numpy as jnp
from jax import lax
from jax.experimental import pallas as pl
from jax.experimental.pallas import tpu as pltpu
from jax.sharding import PartitionSpec as P

rate_alpha = 0.5
rate_beta = 1.0
lasso_weight = 0.5
ridge_weight = 1.0

f32, bf16, i32 = jnp.float32, jnp.bfloat16, jnp.int32
VMEM = pl.BlockSpec(memory_space=pltpu.VMEM)
SMEM = pl.BlockSpec(memory_space=pltpu.SMEM)


def shrink(z_acc, n_acc):
    soft = z_acc - jnp.clip(z_acc, -lasso_weight, lasso_weight)
    return -soft / ((rate_beta + jnp.sqrt(n_acc)) / rate_alpha + ridge_weight)


def iota(shape, dim):
    return lax.broadcasted_iota(i32, shape, dim)


def before(size):
    return (iota((size, size), 0) < iota((size, size), 1)).astype(bf16)


def slot_ids(asked, cap, first, blk):
    parts = asked.shape[1]
    tri = before(128)
    count = None
    picked = None
    for part in range(parts):
        local = asked[:, part, :] - first
        valid = (local >= 0) & (local < blk)
        ones = valid.astype(f32)
        rank = jnp.dot(ones.astype(bf16), tri, preferred_element_type=f32)
        total = jnp.sum(ones, axis=1, keepdims=True)
        if count is not None:
            rank = rank + count
            total = total + count
        count = total
        place = jnp.where(valid, rank.astype(i32), -1)[:, None, :]
        value = (local + 1).astype(f32)[:, None, :]
        shape = (place.shape[0], cap, 128)
        hit = jnp.broadcast_to(place, shape) == iota(shape, 1)
        here = jnp.where(hit, jnp.broadcast_to(value, shape), 0.0)
        picked = here if picked is None else picked + here
    return jnp.sum(picked, axis=2, keepdims=True).astype(i32) - 1


def one_hot_rows(ids, blk):
    rows, cap, _ = ids.shape
    shape = (rows, cap, blk)
    hot = (jnp.broadcast_to(ids, shape) == iota(shape, 2)).astype(f32).astype(bf16)
    return hot.reshape(rows * cap, blk)


def route_kernel(shards, groups, cap, blk, block_ref, group_ref, order_ref, take_ref, put_ref):
    tiles = block_ref.shape[1]
    slots = shards * cap
    tri = before(tiles)
    owner = block_ref[...] // blk
    group = group_ref[...]
    mine = jnp.broadcast_to(owner, (shards, tiles)) == iota((shards, tiles), 0)
    rank = jnp.dot(mine.astype(f32).astype(bf16), tri, preferred_element_type=f32)
    rank = jnp.sum(jnp.where(mine, rank, 0.0), axis=0, keepdims=True)
    inside = jnp.broadcast_to(group, (groups, tiles)) == iota((groups, tiles), 0)
    place = jnp.dot(inside.astype(f32).astype(bf16), tri, preferred_element_type=f32)
    place = place + (iota((groups, tiles), 0) * (tiles // groups)).astype(f32)
    place = jnp.sum(jnp.where(inside, place, 0.0), axis=0, keepdims=True).astype(i32)
    move = (jnp.broadcast_to(place, (tiles, tiles)) == iota((tiles, tiles), 0)).astype(f32)
    slot = owner.astype(f32) * cap + rank
    column = jnp.sum(move * slot, axis=1, keepdims=True).astype(i32)
    take_ref[...] = (jnp.broadcast_to(column, (tiles, slots)) == iota((tiles, slots), 1)).astype(f32).astype(bf16)
    row = iota((8, tiles), 0)
    facts = jnp.where(
        row == 0,
        jnp.broadcast_to(owner.astype(f32), (8, tiles)),
        jnp.where(row == 1, jnp.broadcast_to(rank, (8, tiles)), iota((8, tiles), 1).astype(f32)),
    )
    facts = lax.dot_general(
        facts.astype(bf16), move.astype(bf16), (((1,), (1,)), ((), ())), preferred_element_type=f32
    )
    order_ref[...] = facts[2:3].astype(i32)
    target = (facts[0:1] * cap + facts[1:2]).astype(i32)
    put_ref[...] = (jnp.broadcast_to(target, (slots, tiles)) == iota((slots, tiles), 0)).astype(f32).astype(bf16)


def answer_kernel(shards, cap, asked_ref, z_ref, n_ref, answer_ref):
    blk, lane = z_ref.shape
    me = lax.axis_index("shard")
    rep = lax.axis_index("rep")
    w_pull = shrink(z_ref[...], n_ref[...]).astype(bf16)
    asked = asked_ref[pl.ds(rep * shards, shards)]
    hot = one_hot_rows(slot_ids(asked, cap, me * blk, blk), blk)
    rows = jnp.dot(hot, w_pull, preferred_element_type=f32)
    answer_ref[...] = rows.astype(bf16).reshape(shards, cap, lane)


def state_kernel(cap, asked_ref, z_ref, n_ref, hot_ref, zt_ref, nt_ref):
    blk, lane = z_ref.shape
    half = zt_ref.shape[0]
    me = lax.axis_index("shard")
    rep = lax.axis_index("rep")
    hot_ref[...] = one_hot_rows(slot_ids(asked_ref[...], cap, me * blk, blk), blk)
    zt = z_ref[...].T
    nt = n_ref[...].T
    zt_ref[...] = jnp.where(rep == 0, zt[:half], zt[half:])
    nt_ref[...] = jnp.where(rep == 0, nt[:half], nt[half:])


def worker_kernel(
    shards, cap, order_ref, answer_ref, take_ref, put_ref, labels_ref, tile_ref, margin_ref, out_ref, w_ref, sum_ref, grad_ref
):
    tiles, lane, _ = tile_ref.shape
    groups = labels_ref.shape[0]
    each = tiles // groups
    slots = shards * cap
    w_ref[...] = jnp.dot(take_ref[...], answer_ref[...].reshape(slots, lane), preferred_element_type=f32)
    for g in range(groups):
        def add(j, acc):
            p = g * each + j
            return acc + tile_ref[order_ref[0, p]].astype(f32) * w_ref[pl.ds(p, 1), :]

        sum_ref[g] = lax.fori_loop(0, each, add, jnp.zeros((lane, lane), f32), unroll=8)
    margins = jnp.concatenate([jnp.sum(sum_ref[g], axis=1).reshape(1, lane) for g in range(groups)], axis=0)
    margin_ref[...] = margins
    resid = (jax.nn.sigmoid(margins) - labels_ref[...].astype(f32)).astype(bf16)
    for g in range(groups):
        row = resid[g : g + 1]
        for j in range(0, each, 2):
            p = g * each + j
            pair = jnp.concatenate([tile_ref[order_ref[0, p]], tile_ref[order_ref[0, p + 1]]], axis=1)
            both = jnp.dot(row, pair, preferred_element_type=f32)
            grad_ref[p : p + 1, :] = both[:, :lane]
            grad_ref[p + 1 : p + 2, :] = both[:, lane:]
    sent = jnp.dot(put_ref[...], grad_ref[...].astype(bf16), preferred_element_type=f32)
    half = lane // 2
    out_ref[:shards] = sent[:, :half].astype(bf16).reshape(shards, cap, half)
    out_ref[shards:] = sent[:, half:].astype(bf16).reshape(shards, cap, half)


def update_kernel(incoming_ref, hot_ref, zt_ref, nt_ref, z_out, n_out, w_out):
    sources, cap, half = incoming_ref.shape
    total = lax.dot_general(
        incoming_ref[...].reshape(sources * cap, half),
        hot_ref[...],
        (((0,), (0,)), ((), ())),
        preferred_element_type=f32,
    )
    z_state = zt_ref[...]
    n_state = nt_ref[...]
    w_old = shrink(z_state, n_state)
    new_n = n_state + total * total
    sigma = (jnp.sqrt(new_n) - jnp.sqrt(n_state)) / rate_alpha
    new_z = z_state + total - sigma * w_old
    z_out[...] = new_z
    n_out[...] = new_n
    w_out[...] = shrink(new_z, new_n)


def call(kernel, out, specs, scratch=(), limit=16 << 20):
    return pl.pallas_call(
        kernel,
        out_shape=out,
        in_specs=specs,
        out_specs=jax.tree.map(lambda _: VMEM, out),
        scratch_shapes=list(scratch),
        compiler_params=pltpu.CompilerParams(vmem_limit_bytes=limit),
    )


def body(z_state, n_state, tile_values, tile_block, tile_group, labels):
    blk, lane = z_state.shape
    tiles = tile_block.shape[0]
    groups = labels.shape[0]
    shards = lax.axis_size("shard")
    reps = lax.axis_size("rep")
    half = lane // reps
    need = max(4, (tiles + shards - 2) // (shards - 1))
    cap = (need + 7) // 8 * 8
    slots = shards * cap
    axes = ("rep", "shard")
    shape = jax.ShapeDtypeStruct

    raw = jnp.broadcast_to(tile_block.reshape(1, tiles // 128, 128), (reps * shards, tiles // 128, 128))
    asked = lax.all_to_all(raw, axes, split_axis=0, concat_axis=0, tiled=True)
    order, take, put = call(
        functools.partial(route_kernel, shards, groups, cap, blk),
        (shape((1, tiles), i32), shape((tiles, slots), bf16), shape((slots, tiles), bf16)),
        [VMEM, VMEM],
    )(tile_block.reshape(1, tiles), tile_group.reshape(1, tiles))
    answer = call(
        functools.partial(answer_kernel, shards, cap), shape((shards, cap, lane), bf16), [VMEM] * 3
    )(asked, z_state, n_state)
    answer = lax.all_to_all(answer, "shard", split_axis=0, concat_axis=0, tiled=True)
    hot, zt, nt = call(
        functools.partial(state_kernel, cap),
        (shape((reps * slots, blk), bf16), shape((half, blk), f32), shape((half, blk), f32)),
        [VMEM] * 3,
    )(asked, z_state, n_state)
    margins, outgoing = call(
        functools.partial(worker_kernel, shards, cap),
        (shape((groups, lane), f32), shape((reps * shards, cap, half), bf16)),
        [SMEM] + [VMEM] * 5,
        [pltpu.VMEM((tiles, lane), f32), pltpu.VMEM((groups, lane, lane), f32), pltpu.VMEM((tiles, lane), f32)],
    )(order, answer, take, put, labels, tile_values)
    incoming = lax.all_to_all(outgoing, axes, split_axis=0, concat_axis=0, tiled=True)
    outs = call(update_kernel, (shape((half, blk), f32),) * 3, [VMEM] * 4)(incoming, hot, zt, nt)
    return (margins,) + tuple(o.T for o in outs)


def solution(mesh):
    placed = (
        P("shard", None),
        P("shard", None),
        P(("rep", "shard"), None, None),
        P(("rep", "shard")),
        P(("rep", "shard")),
        P(("rep", "shard"), None),
    )
    return jax.shard_map(
        body,
        mesh=mesh,
        in_specs=placed,
        out_specs=(
            P(("rep", "shard"), None),
            P("shard", "rep"),
            P("shard", "rep"),
            P("shard", "rep"),
        ),
        check_vma=False,
    )
```

time: 103 us -> 51.3 us (0.50)
  waiting for transfers between devices: 39.4 us -> 12.9 us
  matrix products: 14.3 us -> 0 us
  blocking collectives: 0 us -> 14.3 us
  between operations: 14.2 us -> 0.71 us
  starting transfers between devices: 16.7 us -> 6.08 us
  Pallas kernels: 0 us -> 7.85 us
  other arithmetic: 6.56 us -> 0 us
  local copies, waits for them, and re-layouts: 11.2 us -> 8.98 us
    psum x1 -> x0, waiting for transfers between devices: 16.3 us -> none  [from_root(): return lax.psum(kept, axis)]
    all_to_all x0 -> x1, blocking collectives: none -> 14.3 us  [body(): asked = lax.all_to_all(raw, axes, split_axis=0, concat_axis=0, tiled=True)]
    dot_general x3 -> x0, matrix products: 14.3 us -> none  [the longest x1 7.83 us: body(): jnp.einsum('tef,tf->te', tile_values, pulled, preferred_element_type=jnp....]
    all_to_all x3 -> x2, starting transfers between devices: 15.3 us -> 6.08 us  [the longest x1 3.51 us: body(): lax.all_to_all(answer, 'shard', split_axis=0, concat_axis=0, tiled=True)]
    unnamed x8 -> x18, local copies, waits for them, and re-layouts: 0.02 us -> 8.29 us
    all_to_all x3 -> x2, waiting for transfers between devices: 21.1 us -> 12.9 us  [the longest x1 7.1 us: body(): lax.all_to_all(outgoing, axes, split_axis=0, concat_axis=0, tiled=True)]
    pallas_call x0 -> x5, Pallas kernels: none -> 7.85 us  [the longest x1 4.51 us: body(): call(functools.partial(worker_kernel, shards, cap), (shape((groups, lane)...]
    gather x4 -> x0, local copies, waits for them, and re-layouts: 3.12 us -> none  [the longest x2 1.41 us: body(): w_pull[jnp.maximum(asked, 0)]]
  transfers between devices with their start and end apart: 5 -> 2, of which waited for: 5 -> 2; matrix products, arithmetic and copies ran while one was open for 1% -> 0% of each run, Pallas kernels for 0% -> 2%
where the time goes in v1:
time: 51.3 us; the launch traced here: 50.8 us
  blocking collectives  14.3 us (28%)
  waiting for transfers between devices  12.9 us (25%)
  local copies, waits for them, and re-layouts  8.98 us (18%)
  Pallas kernels  7.85 us (15%)
  starting transfers between devices  6.08 us (12%)
  between operations  0.71 us (1%)
    all_to_all x1, blocking collectives, body(): asked = lax.all_to_all(raw, axes, split_axis=0, concat_axis=0, tiled=True)  14.3 us
    unnamed x18, local copies, waits for them, and re-layouts  8.29 us
    all_to_all x1, waiting for transfers between devices, body(): lax.all_to_all(outgoing, axes, split_axis=0, concat_axis=0, tiled=True)  7.1 us
    all_to_all x1, waiting for transfers between devices, body(): lax.all_to_all(answer, 'shard', split_axis=0, concat_axis=0, tiled=True)  5.81 us
    pallas_call x1, Pallas kernels, body(): call(functools.partial(worker_kernel, shards, cap), (shape((groups, lane)...  4.51 us
    all_to_all x1, starting transfers between devices, body(): lax.all_to_all(answer, 'shard', split_axis=0, concat_axis=0, tiled=True)  3.51 us
    all_to_all x1, starting transfers between devices, body(): lax.all_to_all(outgoing, axes, split_axis=0, concat_axis=0, tiled=True)  2.57 us
    pallas_call x1, Pallas kernels, body(): call(functools.partial(answer_kernel, shards, cap), shape((shards, cap, l...  1.21 us
  transfers between devices with their start and end apart: 2, of which 2 were waited for; matrix products, arithmetic and copies ran while one was open for 0% of the time, Pallas kernels for 2%

profile of v1, /device:TPU:0, one launch (start us, length us, event | category | flops | bytes accessed | tf_op | source)
XLA Modules:
  0.0 50.8 jit_solution(11326271461742811446)
XLA Ops:
  0.6 0.7 %broadcast_in_dim.8 = s32[32,2,128]{2,1,0:T(2,128)S(1)} broadcast(s32[2,128]{1,0:T(2,128)} %bitcast.6), dimensions={1,2} | broadcast | bytes 33792 | tf_op jit(solution)/shard_map/broadcast_in_dim | solution.py:192
  1.3 14.3 %all_to_all.15.asked_ref = s32[32,2,128]{2,1,0:T(2,128)S(1)} all-to-all(s32[32,2,128]{2,1,0:T(2,128)S(1)} %broadcast_in_dim.8), channel_id=1, replica_groups=mesh['rep'=2,'shard'=16] {'rep','shard'}, dimensions={0} | all-to-all | bytes 65536 | tf_op jit(solution)/shard_map/all_to_all | solution.py:193
  15.6 0.0 copy-start.1
  15.6 0.9 %copy-done.1 = f32[512,128]{1,0:T(8,128)S(1)} copy-done((f32[512,128]{1,0:T(8,128)S(1)}, f32[512,128]{1,0:T(8,128)}, u32[]{:S(2)}) %copy-start.1) | copy-done | bytes 262168
  16.6 0.0 copy-start.3
  16.6 0.9 %copy-done.3 = f32[512,128]{1,0:T(8,128)S(1)} copy-done((f32[512,128]{1,0:T(8,128)S(1)}, f32[512,128]{1,0:T(8,128)}, u32[]{:S(2)}) %copy-start.3) | copy-done | bytes 262168
  17.5 0.0 copy-start.2
  17.5 0.0 copy-start.4
  17.5 1.2 %shard_map.94 = bf16[16,24,128]{2,1,0:T(8,128)(2,1)} custom-call(s32[32,2,128]{2,1,0:T(2,128)S(1)} %all_to_all.15.asked_ref, f32[512,128]{1,0:T(8,128)S(1)} %copy-done.1, f32[512,128]{1,0:T(8,128)S(1)} %copy-done.3), custom_call_target="tpu_custom_call" | custom-call | tf_op jit(solution)/shard_map/pallas_call | solution.py:199
  18.8 3.5 %all-to-all-start.1 = ((bf16[16,24,128]{2,1,0:T(8,128)(2,1)}), bf16[16,24,128]{2,1,0:T(8,128)(2,1)S(1)}, u32[]{:S(2)}, u32[]{:S(2)}) async-start(bf16[16,24,128]{2,1,0:T(8,128)(2,1)} %shard_map.94), calls=%async_computation.1 | async-start | bytes 196608 | tf_op jit(solution)/shard_map/all_to_all | solution.py:202
  22.3 0.0 copy-start.6
  22.3 0.7 %copy-done.6 = s32[256]{0:T(256)S(1)} copy-done((s32[256]{0:T(256)S(1)}, s32[256]{0:T(256)}, u32[]{:S(2)}) %copy-start.6) | copy-done | bytes 1048
  22.9 0.0 copy-start.7
  22.9 0.7 %copy-done.7 = s32[256]{0:T(256)S(1)} copy-done((s32[256]{0:T(256)S(1)}, s32[256]{0:T(256)}, u32[]{:S(2)}) %copy-start.7) | copy-done | bytes 1048
  23.6 0.5 shard_map.93
  24.1 5.8 %all-to-all-done.1.answer_ref = bf16[16,24,128]{2,1,0:T(8,128)(2,1)S(1)} async-done(((bf16[16,24,128]{2,1,0:T(8,128)(2,1)}), bf16[16,24,128]{2,1,0:T(8,128)(2,1)S(1)}, u32[]{:S(2)}, u32[]{:S(2)}) %all-to-all-start.1) | async-done | bytes 98336 | tf_op jit(solution)/shard_map/all_to_all | solution.py:202
  29.9 0.0 copy-start
  29.9 3.4 %copy-done = bf16[256,128,128]{2,1,0:T(8,128)(2,1)S(1)} copy-done((bf16[256,128,128]{2,1,0:T(8,128)(2,1)S(1)}, bf16[256,128,128]{2,1,0:T(8,128)(2,1)}, u32[]{:S(2)}) %copy-start) | copy-done | bytes 8388632
  33.3 0.0 copy-start.5
  33.3 0.7 %copy-done.5 = s32[8,128]{1,0:T(8,128)S(1)} copy-done((s32[8,128]{1,0:T(8,128)S(1)}, s32[8,128]{1,0:T(8,128)}, u32[]{:S(2)}) %copy-start.5) | copy-done | bytes 4120
  34.0 4.5 %shard_map.95 = (f32[8,128]{1,0:T(8,128)}, bf16[32,24,64]{2,1,0:T(8,128)(2,1)S(1)}) custom-call(s32[1,256]{1,0:T(1,128)S(1)} %get-tuple-element.15.order_ref, bf16[16,24,128]{2,1,0:T(8,128)(2,1)S(1)} %all-to-all-done.1.answer_ref, bf16[256,384]{1,0:T(8,128)(2,1)S(1)} %get-tuple-element.16.take_ref, bf16[384,256]{1,0:T(8,128)(2,1)S(1)} %get-tuple-element.17.put_ref, ...), custom_call_target="tpu_custom_call" | custom-call | tf_op jit(solution)/shard_map/pallas_call | solution.py:208
  38.5 0.8 %reshape.18 = bf16[32,2,768]{2,1,0:T(2,128)(2,1)} reshape(bf16[32,24,64]{2,1,0:T(8,128)(2,1)S(1)} %get-tuple-element.19) | data formatting | bytes 196608
  39.3 2.6 %all-to-all-start.2 = ((bf16[32,2,768]{2,1,0:T(2,128)(2,1)}), bf16[32,2,768]{2,1,0:T(2,128)(2,1)S(1)}, u32[]{:S(2)}, u32[]{:S(2)}) async-start(bf16[32,2,768]{2,1,0:T(2,128)(2,1)} %reshape.18), calls=%async_computation.2 | async-start | bytes 196608 | tf_op jit(solution)/shard_map/all_to_all | solution.py:214
  41.9 0.0 copy-done.2
  41.9 0.0 copy-done.4
  41.9 0.6 %shard_map.96 = (bf16[768,512]{1,0:T(8,128)(2,1)S(1)}, f32[64,512]{1,0:T(8,128)S(1)}, f32[64,512]{1,0:T(8,128)S(1)}) custom-call(s32[32,2,128]{2,1,0:T(2,128)S(1)} %all_to_all.15.asked_ref, f32[512,128]{1,0:T(8,128)S(1)} %copy-done.2, f32[512,128]{1,0:T(8,128)S(1)} %copy-done.4), custom_call_target="tpu_custom_call" | custom-call | tf_op jit(solution)/shard_map/pallas_call | solution.py:203
  42.4 7.1 %all-to-all-done.2 = bf16[32,2,768]{2,1,0:T(2,128)(2,1)S(1)} async-done(((bf16[32,2,768]{2,1,0:T(2,128)(2,1)}), bf16[32,2,768]{2,1,0:T(2,128)(2,1)S(1)}, u32[]{:S(2)}, u32[]{:S(2)}) %all-to-all-start.2) | async-done | bytes 98336 | tf_op jit(solution)/shard_map/all_to_all | solution.py:214
  49.5 0.2 reshape.19.incoming_ref
  49.7 1.1 %shard_map.97 = (f32[64,512]{1,0:T(8,128)}, f32[64,512]{1,0:T(8,128)}, f32[64,512]{1,0:T(8,128)}) custom-call(bf16[32,24,64]{2,1,0:T(8,128)(2,1)S(1)} %reshape.19.incoming_ref, bf16[768,512]{1,0:T(8,128)(2,1)S(1)} %get-tuple-element.20.hot_ref, f32[64,512]{1,0:T(8,128)S(1)} %get-tuple-element.21.zt_ref, f32[64,512]{1,0:T(8,128)S(1)} %get-tuple-element.22.nt_ref), custom_call_target="tpu_custom_call" | custom-call | tf_op jit(solution)/shard_map/pallas_call | solution.py:215
Async XLA Ops:
  15.6 1.0 %copy-start.1 = (f32[512,128]{1,0:T(8,128)S(1)}, f32[512,128]{1,0:T(8,128)}, u32[]{:S(2)}) copy-start(f32[512,128]{1,0:T(8,128)} %z_ref.3) | copy-start | bytes 786436
  16.6 0.9 %copy-start.3 = (f32[512,128]{1,0:T(8,128)S(1)}, f32[512,128]{1,0:T(8,128)}, u32[]{:S(2)}) copy-start(f32[512,128]{1,0:T(8,128)} %n_ref.3) | copy-start | bytes 786436
  17.5 24.3 %copy-start.2 = (f32[512,128]{1,0:T(8,128)S(1)}, f32[512,128]{1,0:T(8,128)}, u32[]{:S(2)}) copy-start(f32[512,128]{1,0:T(8,128)} %z_ref.3) | copy-start | bytes 786436
  17.5 24.3 %copy-start.4 = (f32[512,128]{1,0:T(8,128)S(1)}, f32[512,128]{1,0:T(8,128)}, u32[]{:S(2)}) copy-start(f32[512,128]{1,0:T(8,128)} %n_ref.3) | copy-start | bytes 786436
  18.8 11.1 %all-to-all-start.1 = ((bf16[16,24,128]{2,1,0:T(8,128)(2,1)}), bf16[16,24,128]{2,1,0:T(8,128)(2,1)S(1)}, u32[]{:S(2)}, u32[]{:S(2)}) async-start(bf16[16,24,128]{2,1,0:T(8,128)(2,1)} %shard_map.94), calls=%async_computation.1 | async-start | bytes 196608 | tf_op jit(solution)/shard_map/all_to_all | solution.py:202
  22.3 0.7 %copy-start.6 = (s32[256]{0:T(256)S(1)}, s32[256]{0:T(256)}, u32[]{:S(2)}) copy-start(s32[256]{0:T(256)} %param.9) | copy-start | bytes 3076
  22.9 0.7 %copy-start.7 = (s32[256]{0:T(256)S(1)}, s32[256]{0:T(256)}, u32[]{:S(2)}) copy-start(s32[256]{0:T(256)} %param.10) | copy-start | bytes 3076
  29.9 3.4 %copy-start = (bf16[256,128,128]{2,1,0:T(8,128)(2,1)S(1)}, bf16[256,128,128]{2,1,0:T(8,128)(2,1)}, u32[]{:S(2)}) copy-start(bf16[256,128,128]{2,1,0:T(8,128)(2,1)} %tile_ref.1) | copy-start | bytes 25165828
  33.3 0.7 %copy-start.5 = (s32[8,128]{1,0:T(8,128)S(1)}, s32[8,128]{1,0:T(8,128)}, u32[]{:S(2)}) copy-start(s32[8,128]{1,0:T(8,128)} %labels_ref.1) | copy-start | bytes 12292
  39.3 10.3 %all-to-all-start.2 = ((bf16[32,2,768]{2,1,0:T(2,128)(2,1)}), bf16[32,2,768]{2,1,0:T(2,128)(2,1)S(1)}, u32[]{:S(2)}, u32[]{:S(2)}) async-start(bf16[32,2,768]{2,1,0:T(2,128)(2,1)} %reshape.18), calls=%async_computation.2 | async-start | bytes 196608 | tf_op jit(solution)/shard_map/all_to_all | solution.py:214

commit v2 on v1

v2 whole, which is shorter than its diff:
```python
import functools

import jax
import jax.numpy as jnp
from jax import lax
from jax.experimental import pallas as pl
from jax.experimental.pallas import tpu as pltpu
from jax.sharding import PartitionSpec as P

rate_alpha = 0.5
rate_beta = 1.0
lasso_weight = 0.5
ridge_weight = 1.0

f32, bf16, i32 = jnp.float32, jnp.bfloat16, jnp.int32
VMEM = pl.BlockSpec(memory_space=pltpu.VMEM)
SMEM = pl.BlockSpec(memory_space=pltpu.SMEM)
HBM = pl.BlockSpec(memory_space=pltpu.HBM)
INNER = 4


def shrink(z_acc, n_acc):
    soft = z_acc - jnp.clip(z_acc, -lasso_weight, lasso_weight)
    return -soft / ((rate_beta + jnp.sqrt(n_acc)) / rate_alpha + ridge_weight)


def iota(shape, dim):
    return lax.broadcasted_iota(i32, shape, dim)


def mask(hit):
    return hit.astype(f32).astype(bf16)


def before(size):
    return mask(iota((size, size), 0) < iota((size, size), 1))


def pull_kernel(z_hbm, n_hbm, pull_ref, z_ref, n_ref, sem):
    z_copy = pltpu.make_async_copy(z_hbm, z_ref, sem.at[0])
    n_copy = pltpu.make_async_copy(n_hbm, n_ref, sem.at[1])
    z_copy.start()
    n_copy.start()
    z_copy.wait()
    n_copy.wait()
    pull_ref[...] = shrink(z_ref[...], n_ref[...]).astype(bf16)


def route_kernel(shards, groups, cap, room, relative, blk, block_ref, group_ref, order_ref, take_ref, put_ref, code_ref):
    tiles = block_ref.shape[1]
    outers = shards // INNER
    base = lax.axis_index("shard") // INNER if relative else 0
    tri = before(tiles)
    block = block_ref[...]
    owner = block // blk
    local = block - owner * blk + 1
    group = group_ref[...]

    def rank_in(key, count):
        same = jnp.broadcast_to(key, (count, tiles)) == iota((count, tiles), 0)
        rank = jnp.dot(mask(same), tri, preferred_element_type=f32)
        return jnp.sum(jnp.where(same, rank, 0.0), axis=0, keepdims=True)

    outer = (owner // INNER) ^ base
    answer_rank = rank_in(outer, outers)
    send_rank = rank_in(owner, shards)
    place = (group * (tiles // groups)).astype(f32) + rank_in(group, groups)
    move = (jnp.broadcast_to(place.astype(i32), (tiles, tiles)) == iota((tiles, tiles), 0)).astype(f32)
    slot = outer.astype(f32) * room + answer_rank
    column = jnp.sum(move * slot, axis=1, keepdims=True).astype(i32)
    take_ref[...] = mask(jnp.broadcast_to(column, (tiles, outers * room)) == iota((tiles, outers * room), 1))
    row = iota((8, tiles), 0)
    facts = jnp.where(
        row == 0,
        jnp.broadcast_to(owner.astype(f32), (8, tiles)),
        jnp.where(row == 1, jnp.broadcast_to(send_rank, (8, tiles)), iota((8, tiles), 1).astype(f32)),
    )
    facts = lax.dot_general(
        facts.astype(bf16), move.astype(bf16), (((1,), (1,)), ((), ())), preferred_element_type=f32
    )
    order_ref[...] = facts[2:3].astype(i32)
    target = (facts[0:1] * cap + facts[1:2]).astype(i32)
    put_ref[...] = mask(jnp.broadcast_to(target, (shards * cap, tiles)) == iota((shards * cap, tiles), 0))
    number = jnp.sum(move * local.astype(f32), axis=1, keepdims=True).astype(i32)
    lane = code_ref.shape[1]
    at = iota((tiles, lane), 1) - lane // 2
    low = jnp.broadcast_to((number % 256).astype(f32), (tiles, lane))
    high = jnp.broadcast_to((number // 256).astype(f32), (tiles, lane))
    code_ref[...] = jnp.where(at == 0, low, jnp.where(at == 1, high, 0.0)).astype(bf16)


def answer_kernel(asked_count, room, *refs):
    asked_refs = refs[:asked_count]
    table_refs = refs[asked_count : asked_count + INNER]
    out_refs = refs[asked_count + INNER :]
    blk, lane = table_refs[0].shape
    parts = asked_refs[0].shape[-2]
    me = lax.axis_index("shard")
    inner = me % INNER
    outer = me // INNER
    tri = before(128)
    count = None
    picked = None
    for part in range(parts):
        if asked_refs[0].ndim == 3:
            block = asked_refs[0][:, part, :]
        else:
            block = jnp.concatenate([r[part : part + 1, :] for r in asked_refs], axis=0)
        owner = block // blk
        valid = owner // INNER == outer
        ones = valid.astype(f32)
        rank = jnp.dot(ones.astype(bf16), tri, preferred_element_type=f32)
        total = jnp.sum(ones, axis=1, keepdims=True)
        if count is not None:
            rank = rank + count
            total = total + count
        count = total
        row = ((owner % INNER) ^ inner) * blk + (block - owner * blk)
        place = jnp.where(valid, rank.astype(i32), -1)[:, None, :]
        value = (row + 1).astype(f32)[:, None, :]
        shape = (place.shape[0], room, 128)
        hit = jnp.broadcast_to(place, shape) == iota(shape, 1)
        here = jnp.where(hit, jnp.broadcast_to(value, shape), 0.0)
        picked = here if picked is None else picked + here
    ids = jnp.sum(picked, axis=2, keepdims=True).astype(i32) - 1
    askers = ids.shape[0]
    shape = (askers, room, blk)
    rows = None
    for j in range(INNER):
        hot = mask(jnp.broadcast_to(ids - j * blk, shape) == iota(shape, 2)).reshape(askers * room, blk)
        term = jnp.dot(hot, table_refs[j][...], preferred_element_type=f32)
        rows = term if rows is None else rows + term
    rows = rows.astype(bf16)
    if out_refs[0].ndim == 3:
        out_refs[0][...] = rows.reshape(askers, room, lane)
    else:
        for k, out_ref in enumerate(out_refs):
            out_ref[...] = rows[k * room : (k + 1) * room]


def state_kernel(z_ref, n_ref, zt_ref, nt_ref):
    half = zt_ref.shape[0]
    rep = lax.axis_index("rep")
    zt = z_ref[...].T
    nt = n_ref[...].T
    zt_ref[...] = jnp.where(rep == 0, zt[:half], zt[half:])
    nt_ref[...] = jnp.where(rep == 0, nt[:half], nt[half:])


def worker_kernel(
    shards, cap, answers, order_ref, take_ref, put_ref, code_ref, labels_ref, tile_ref, *refs
):
    answer_refs = refs[:answers]
    margin_ref, out_ref, w_ref, sum_ref, grad_ref = refs[answers:]
    tiles, lane, _ = tile_ref.shape
    groups = labels_ref.shape[0]
    each = tiles // groups
    answer = [r[...].reshape(-1, lane) for r in answer_refs]
    answer = answer[0] if answers == 1 else jnp.concatenate(answer, axis=0)
    w_ref[...] = jnp.dot(take_ref[...], answer, preferred_element_type=f32)
    for g in range(groups):
        def add(j, acc):
            p = g * each + j
            return acc + tile_ref[order_ref[0, p]].astype(f32) * w_ref[pl.ds(p, 1), :]

        sum_ref[g] = lax.fori_loop(0, each, add, jnp.zeros((lane, lane), f32), unroll=8)
    margins = jnp.concatenate([jnp.sum(sum_ref[g], axis=1).reshape(1, lane) for g in range(groups)], axis=0)
    margin_ref[...] = margins
    resid = (jax.nn.sigmoid(margins) - labels_ref[...].astype(f32)).astype(bf16)
    for g in range(groups):
        row = resid[g : g + 1]
        for j in range(0, each, 2):
            p = g * each + j
            pair = jnp.concatenate([tile_ref[order_ref[0, p]], tile_ref[order_ref[0, p + 1]]], axis=1)
            both = jnp.dot(row, pair, preferred_element_type=f32)
            grad_ref[p : p + 1, :] = both[:, :lane]
            grad_ref[p + 1 : p + 2, :] = both[:, lane:]
    grads = grad_ref[...]
    half = lane // 2
    left = iota((tiles, lane), 1) < half
    code = code_ref[...].astype(f32)
    put = put_ref[...]
    for rep in range(2):
        side = grads if rep == 0 else jnp.concatenate([grads[:, half:], grads[:, :half]], axis=1)
        side = jnp.where(left, side, code).astype(bf16)
        sent = jnp.dot(put, side, preferred_element_type=f32).astype(bf16)
        out_ref[rep * shards : (rep + 1) * shards] = sent.reshape(shards, cap, lane)


def update_kernel(incoming_ref, zt_ref, nt_ref, z_out, n_out, w_out):
    sources, cap, lane = incoming_ref.shape
    half, blk = zt_ref.shape
    rows = sources * cap
    incoming = incoming_ref[...].reshape(rows, lane)
    low = incoming[:, half : half + 1].astype(f32)
    high = incoming[:, half + 1 : half + 2].astype(f32)
    ids = (low + high * 256.0).astype(i32) - 1
    hot = mask(jnp.broadcast_to(ids, (rows, blk)) == iota((rows, blk), 1))
    total = lax.dot_general(incoming, hot, (((0,), (0,)), ((), ())), preferred_element_type=f32)[:half]
    z_state = zt_ref[...]
    n_state = nt_ref[...]
    w_old = shrink(z_state, n_state)
    new_n = n_state + total * total
    sigma = (jnp.sqrt(new_n) - jnp.sqrt(n_state)) / rate_alpha
    new_z = z_state + total - sigma * w_old
    z_out[...] = new_z
    n_out[...] = new_n
    w_out[...] = shrink(new_z, new_n)


def call(kernel, out, specs, scratch=(), limit=16 << 20, flops=0):
    return pl.pallas_call(
        kernel,
        out_shape=out,
        in_specs=specs,
        out_specs=jax.tree.map(lambda _: VMEM, out),
        scratch_shapes=list(scratch),
        compiler_params=pltpu.CompilerParams(vmem_limit_bytes=limit),
        cost_estimate=pl.CostEstimate(flops=flops, bytes_accessed=0, transcendentals=0),
    )


def crossed(x, by):
    size = lax.axis_size("shard")
    return lax.ppermute(x, "shard", [(i, i ^ by) for i in range(size)])


def body(z_state, n_state, tile_values, tile_block, tile_group, labels):
    blk, lane = z_state.shape
    tiles = tile_block.shape[0]
    groups = labels.shape[0]
    shards = lax.axis_size("shard")
    reps = lax.axis_size("rep")
    half = lane // reps
    outers = shards // INNER
    need = max(4, (tiles + shards - 2) // (shards - 1))
    cap = (need + 7) // 8 * 8
    room = (min(INNER * need, tiles) + 15) // 16 * 16
    relative = outers <= 4
    shape = jax.ShapeDtypeStruct

    ids = tile_block.reshape(tiles // 128, 128)
    pull = call(
        pull_kernel,
        shape((blk, lane), bf16),
        [HBM] * 2,
        [pltpu.VMEM((blk, lane), f32)] * 2 + [pltpu.SemaphoreType.DMA((2,))],
        limit=(64 << 20) - 5 * blk * lane // 2,
    )(z_state, n_state)
    if relative:
        asked = [crossed(ids, INNER * k) for k in range(1, outers)]
    else:
        columns = [[b * INNER + a for b in range(outers)] for a in range(INNER)]
        swap = functools.partial(
            lax.all_to_all, axis_name="shard", split_axis=0, concat_axis=0, tiled=True, axis_index_groups=columns
        )
        asked = [swap(jnp.broadcast_to(ids[None], (outers,) + ids.shape))]
    table = [pull] + [crossed(pull, j) for j in range(1, INNER)]

    order, take, put, code = call(
        functools.partial(route_kernel, shards, groups, cap, room, relative, blk),
        (
            shape((1, tiles), i32),
            shape((tiles, outers * room), bf16),
            shape((shards * cap, tiles), bf16),
            shape((tiles, lane), bf16),
        ),
        [VMEM, VMEM],
        flops=8 * 10**9,
    )(tile_block.reshape(1, tiles), tile_group.reshape(1, tiles))
    zt, nt = call(state_kernel, (shape((half, blk), f32),) * 2, [VMEM] * 2)(z_state, n_state)

    def answered(asked, out):
        return call(
            functools.partial(answer_kernel, len(asked), room), out, [VMEM] * (len(asked) + INNER)
        )(*asked, *table)

    if relative:
        replies = answered(asked, (shape((room, lane), bf16),) * (outers - 1))
        answers = [crossed(reply, INNER * (k + 1)) for k, reply in enumerate(replies)]
        answers = list(answered([ids], (shape((room, lane), bf16),))) + answers
    else:
        answers = [swap(answered(asked, shape((outers, room, lane), bf16)))]
    margins, outgoing = call(
        functools.partial(worker_kernel, shards, cap, len(answers)),
        (shape((groups, lane), f32), shape((reps * shards, cap, lane), bf16)),
        [SMEM] + [VMEM] * (5 + len(answers)),
        [pltpu.VMEM((tiles, lane), f32), pltpu.VMEM((groups, lane, lane), f32), pltpu.VMEM((tiles, lane), f32)],
    )(order, take, put, code, labels, tile_values, *answers)
    incoming = lax.all_to_all(outgoing, ("rep", "shard"), split_axis=0, concat_axis=0, tiled=True)
    outs = call(update_kernel, (shape((half, blk), f32),) * 3, [VMEM] * 3)(incoming, zt, nt)
    return (margins,) + tuple(o.T for o in outs)


def solution(mesh):
    placed = (
        P("shard", None),
        P("shard", None),
        P(("rep", "shard"), None, None),
        P(("rep", "shard")),
        P(("rep", "shard")),
        P(("rep", "shard"), None),
    )
    return jax.shard_map(
        body,
        mesh=mesh,
        in_specs=placed,
        out_specs=(
            P(("rep", "shard"), None),
            P("shard", "rep"),
            P("shard", "rep"),
            P("shard", "rep"),
        ),
        check_vma=False,
    )
```

time: 51.3 us -> 48.8 us (0.951)
  starting transfers between devices: 6.08 us -> 20.9 us
  blocking collectives: 14.3 us -> 0 us
  local copies, waits for them, and re-layouts: 8.98 us -> 2.64 us
  Pallas kernels: 7.85 us -> 10.1 us
  waiting for transfers between devices: 12.9 us -> 14.2 us
    ppermute x0 -> x9, starting transfers between devices: none -> 16.8 us  [crossed(): return lax.ppermute(x, 'shard', [(i, i ^ by) for i in range(size)])]
    all_to_all x1 -> x0, blocking collectives: 14.3 us -> none  [body(): asked = lax.all_to_all(raw, axes, split_axis=0, concat_axis=0, tiled=True)]
    unnamed x18 -> x20, local copies, waits for them, and re-layouts: 8.29 us -> 2.64 us
    ppermute x0 -> x9, waiting for transfers between devices: none -> 4.58 us  [crossed(): return lax.ppermute(x, 'shard', [(i, i ^ by) for i in range(size)])]
    all_to_all x2 -> x1, waiting for transfers between devices: 12.9 us -> 9.58 us  [body(): lax.all_to_all(outgoing, ('rep', 'shard'), split_axis=0, concat_axis=0, t...]
    pallas_call x5 -> x7, Pallas kernels: 7.85 us -> 10.1 us  [the longest x1 5.06 us: body(): call(functools.partial(worker_kernel, shards, cap, len(answers)), (shape(...]
    all_to_all x2 -> x1, starting transfers between devices: 6.08 us -> 4.1 us  [body(): lax.all_to_all(outgoing, ('rep', 'shard'), split_axis=0, concat_axis=0, t...]
    broadcast_in_dim x1 -> x0, local copies, waits for them, and re-layouts: 0.69 us -> none  [body(): jnp.broadcast_to(tile_block.reshape(1, tiles // 128, 128), (reps * shards...]
  transfers between devices with their start and end apart: 2 -> 10, of which waited for: 2 -> 3; matrix products, arithmetic and copies ran while one was open for 0% -> 0% of each run, Pallas kernels for 2% -> 2%
where the time goes in v2:
time: 48.8 us; the launch traced here: 48.6 us
  starting transfers between devices  20.9 us (43%)
  waiting for transfers between devices  14.2 us (29%)
  Pallas kernels  10.1 us (21%)
  local copies, waits for them, and re-layouts  2.64 us (5%)
  between operations  0.75 us (2%)
    ppermute x9, starting transfers between devices, crossed(): return lax.ppermute(x, 'shard', [(i, i ^ by) for i in range(size)])  16.8 us
    all_to_all x1, waiting for transfers between devices, body(): lax.all_to_all(outgoing, ('rep', 'shard'), split_axis=0, concat_axis=0, t...  9.58 us
    pallas_call x1, Pallas kernels, body(): call(functools.partial(worker_kernel, shards, cap, len(answers)), (shape(...  5.06 us
    ppermute x9, waiting for transfers between devices, crossed(): return lax.ppermute(x, 'shard', [(i, i ^ by) for i in range(size)])  4.58 us
    all_to_all x1, starting transfers between devices, body(): lax.all_to_all(outgoing, ('rep', 'shard'), split_axis=0, concat_axis=0, t...  4.1 us
    unnamed x20, local copies, waits for them, and re-layouts  2.64 us
    pallas_call x1, Pallas kernels, body(): call(pull_kernel, shape((blk, lane), bf16), [HBM] * 2, [pltpu.VMEM((blk,...  1.84 us
    pallas_call x1, Pallas kernels, body(): call(update_kernel, (shape((half, blk), f32),) * 3, [VMEM] * 3)  1.36 us
  transfers between devices with their start and end apart: 10, of which 3 were waited for; matrix products, arithmetic and copies ran while one was open for 0% of the time, Pallas kernels for 2%

profile of v2, /device:TPU:0, one launch (start us, length us, event | category | flops | bytes accessed | tf_op | source)
XLA Modules:
  0.0 48.6 jit_solution(14172913011793514145)
XLA Ops:
  0.6 1.8 %shard_map.94.refs_1_.refs_3_ = bf16[512,128]{1,0:T(8,128)(2,1)} custom-call(f32[512,128]{1,0:T(8,128)} %z_ref.1, f32[512,128]{1,0:T(8,128)} %n_ref.1), custom_call_target="tpu_custom_call" | custom-call | tf_op jit(solution)/shard_map/pallas_call | solution.py:243
  2.5 3.0 %collective-permute-start = (bf16[512,128]{1,0:T(8,128)(2,1)}, bf16[512,128]{1,0:T(8,128)(2,1)S(1)}, u32[]{:S(2)}, u32[]{:S(2)}) collective-permute-start(bf16[512,128]{1,0:T(8,128)(2,1)} %shard_map.94.refs_1_.refs_3_), channel_id=1, source_target_pairs={{0,1},{1,0},{2,3},{3,2},{4,5},{5,4},{6,7},{7,6},{8,9},{9,8},{10,11... | collective-permute-start | bytes 393224 | tf_op jit(solution)/shard_map/ppermute | solution.py:225
  5.5 1.5 %collective-permute-start.1 = (bf16[512,128]{1,0:T(8,128)(2,1)}, bf16[512,128]{1,0:T(8,128)(2,1)S(1)}, u32[]{:S(2)}, u32[]{:S(2)}) collective-permute-start(bf16[512,128]{1,0:T(8,128)(2,1)} %shard_map.94.refs_1_.refs_3_), channel_id=1, source_target_pairs={{0,2},{1,3},{2,0},{3,1},{4,6},{5,7},{6,4},{7,5},{8,10},{9,11},{10,... | collective-permute-start | bytes 393224 | tf_op jit(solution)/shard_map/ppermute | solution.py:225
  7.0 0.0 collective-permute-start.2
  7.0 2.0 %collective-permute-start.3 = (s32[2,128]{1,0:T(2,128)}, s32[2,128]{1,0:T(2,128)S(1)}, u32[]{:S(2)}, u32[]{:S(2)}) collective-permute-start(s32[2,128]{1,0:T(2,128)} %bitcast.8), channel_id=1, source_target_pairs={{0,4},{1,5},{2,6},{3,7},{4,0},{5,1},{6,2},{7,3},{8,12},{9,13},{10,... | collective-permute-start | bytes 3080 | tf_op jit(solution)/shard_map/ppermute | solution.py:225
  9.1 2.6 %collective-permute-start.4 = (s32[2,128]{1,0:T(2,128)}, s32[2,128]{1,0:T(2,128)S(1)}, u32[]{:S(2)}, u32[]{:S(2)}) collective-permute-start(s32[2,128]{1,0:T(2,128)} %bitcast.9), channel_id=1, source_target_pairs={{0,8},{1,9},{2,10},{3,11},{4,12},{5,13},{6,14},{7,15},{8,0},{9,1},... | collective-permute-start | bytes 3080 | tf_op jit(solution)/shard_map/ppermute | solution.py:225
  11.6 0.0 collective-permute-done.3.refs_0_
  11.7 3.2 %collective-permute-start.5 = (s32[2,128]{1,0:T(2,128)}, s32[2,128]{1,0:T(2,128)S(1)}, u32[]{:S(2)}, u32[]{:S(2)}) collective-permute-start(s32[2,128]{1,0:T(2,128)} %bitcast.10), channel_id=1, source_target_pairs={{0,12},{1,13},{2,14},{3,15},{4,8},{5,9},{6,10},{7,11},{8,4},{9,5},... | collective-permute-start | bytes 3080 | tf_op jit(solution)/shard_map/ppermute | solution.py:225
  14.9 0.0 collective-permute-done.4.refs_1_
  14.9 2.4 %collective-permute-done.5.refs_2_ = s32[2,128]{1,0:T(2,128)S(1)} collective-permute-done((s32[2,128]{1,0:T(2,128)}, s32[2,128]{1,0:T(2,128)S(1)}, u32[]{:S(2)}, u32[]{:S(2)}) %collective-permute-start.5) | collective-permute-done | bytes 1056 | tf_op jit(solution)/shard_map/ppermute | solution.py:225
  17.2 0.0 collective-permute-done.refs_2_.refs_4_
  17.2 0.0 collective-permute-done.1.refs_3_.refs_5_
  17.2 0.0 collective-permute-done.2.refs_4_.refs_6_
  17.2 0.0 copy-start
  17.3 0.9 %copy-done = bf16[512,128]{1,0:T(8,128)(2,1)S(1)} copy-done((bf16[512,128]{1,0:T(8,128)(2,1)S(1)}, bf16[512,128]{1,0:T(8,128)(2,1)}, u32[]{:S(2)}) %copy-start) | copy-done | bytes 131096
  18.2 0.0 slice-start
  18.2 0.6 %shard_map.96 = (bf16[80,128]{1,0:T(8,128)(2,1)S(1)}, bf16[80,128]{1,0:T(8,128)(2,1)S(1)}, bf16[80,128]{1,0:T(8,128)(2,1)S(1)}) custom-call(s32[2,128]{1,0:T(2,128)S(1)} %collective-permute-done.3.refs_0_, s32[2,128]{1,0:T(2,128)S(1)} %collective-permute-done.4.refs_1_, s32[2,128]{1,0:T(2,128)S(1)} %collective-permute-done.5.refs_2_, ...), custom_call_target="tpu_custom_call" | custom-call | tf_op jit(solution)/shard_map/pallas_call | solution.py:274
  18.8 0.1 collective-permute-start.6
  18.9 3.8 %collective-permute-start.7 = (bf16[80,128]{1,0:T(8,128)(2,1)S(1)}, bf16[80,128]{1,0:T(8,128)(2,1)S(1)}, u32[]{:S(2)}, u32[]{:S(2)}) collective-permute-start(bf16[80,128]{1,0:T(8,128)(2,1)S(1)} %get-tuple-element.23), channel_id=1, source_target_pairs={{0,8},{1,9},{2,10},{3,11},{4,12},{5,13},{6,14},{7,15},{8,0},{9,1},... | collective-permute-start | bytes 61448 | tf_op jit(solution)/shard_map/ppermute | solution.py:225
  22.6 0.6 %collective-permute-start.8 = (bf16[80,128]{1,0:T(8,128)(2,1)S(1)}, bf16[80,128]{1,0:T(8,128)(2,1)S(1)}, u32[]{:S(2)}, u32[]{:S(2)}) collective-permute-start(bf16[80,128]{1,0:T(8,128)(2,1)S(1)} %get-tuple-element.24), channel_id=1, source_target_pairs={{0,12},{1,13},{2,14},{3,15},{4,8},{5,9},{6,10},{7,11},{8,4},{9,5},... | collective-permute-start | bytes 61448 | tf_op jit(solution)/shard_map/ppermute | solution.py:225
  23.2 0.0 copy-start.5
  23.2 0.7 %copy-done.5 = s32[256]{0:T(256)S(1)} copy-done((s32[256]{0:T(256)S(1)}, s32[256]{0:T(256)}, u32[]{:S(2)}) %copy-start.5) | copy-done | bytes 1048
  23.9 0.0 copy-start.7
  23.9 0.7 %copy-done.7 = s32[256]{0:T(256)S(1)} copy-done((s32[256]{0:T(256)S(1)}, s32[256]{0:T(256)}, u32[]{:S(2)}) %copy-start.7) | copy-done | bytes 1048
  24.6 0.0 copy-start.1
  24.6 0.0 copy-start.6
  24.6 0.0 slice-start.1
  24.6 0.0 copy-start.4
  24.6 0.5 %shard_map.93 = (s32[1,256]{1,0:T(1,128)S(1)}, bf16[256,320]{1,0:T(8,128)(2,1)S(1)}, bf16[384,256]{1,0:T(8,128)(2,1)S(1)}, bf16[256,128]{1,0:T(8,128)(2,1)S(1)}) custom-call(s32[1,256]{1,0:T(1,128)S(1)} %bitcast.11, s32[1,256]{1,0:T(1,128)S(1)} %bitcast.13), custom_call_target="tpu_custom_call" | custom-call | flops 8000000000 | tf_op jit(solution)/shard_map/pallas_call | solution.py:260
  25.1 0.4 copy-done.1
  25.5 0.0 copy-done.6
  25.5 0.0 copy-start.2
  25.5 0.0 copy-start.3
  25.5 0.5 shard_map.95.refs_0_
  26.0 0.0 collective-permute-done.6.refs_1_
  26.0 0.0 collective-permute-done.7.refs_2_
  26.0 2.2 %collective-permute-done.8.refs_3_ = bf16[80,128]{1,0:T(8,128)(2,1)S(1)} collective-permute-done((bf16[80,128]{1,0:T(8,128)(2,1)S(1)}, bf16[80,128]{1,0:T(8,128)(2,1)S(1)}, u32[]{:S(2)}, u32[]{:S(2)}) %collective-permute-start.8) | collective-permute-done | bytes 20512 | tf_op jit(solution)/shard_map/ppermute | solution.py:225
  28.2 0.0 slice-done
  28.2 0.0 slice-done.1
  28.2 0.0 copy-done.4
  28.2 5.1 %shard_map.97 = (f32[8,128]{1,0:T(8,128)}, bf16[32,24,128]{2,1,0:T(8,128)(2,1)}) custom-call(s32[1,256]{1,0:T(1,128)S(1)} %get-tuple-element.18.order_ref, bf16[256,320]{1,0:T(8,128)(2,1)S(1)} %get-tuple-element.19.take_ref, bf16[384,256]{1,0:T(8,128)(2,1)S(1)} %get-tuple-element.20.put_ref, bf16[256,128]{1,0:T(8,128)(2,1)S(1)} %get-tuple-element.21.code_ref, ...), custom_call_target="tpu_custom_call" | custom-call | tf_op jit(solution)/shard_map/pallas_call | solution.py:284
  33.3 4.1 %all-to-all-start = ((bf16[32,24,128]{2,1,0:T(8,128)(2,1)}), bf16[32,24,128]{2,1,0:T(8,128)(2,1)S(1)}, u32[]{:S(2)}, u32[]{:S(2)}) async-start(bf16[32,24,128]{2,1,0:T(8,128)(2,1)} %get-tuple-element.26), calls=%async_computation | async-start | bytes 393216 | tf_op jit(solution)/shard_map/all_to_all | solution.py:290
  37.4 0.0 copy-done.2
  37.4 0.0 copy-done.3
  37.4 0.2 shard_map.98
  37.6 9.6 %all-to-all-done.incoming_ref = bf16[32,24,128]{2,1,0:T(8,128)(2,1)S(1)} async-done(((bf16[32,24,128]{2,1,0:T(8,128)(2,1)}), bf16[32,24,128]{2,1,0:T(8,128)(2,1)S(1)}, u32[]{:S(2)}, u32[]{:S(2)}) %all-to-all-start) | async-done | bytes 196640 | tf_op jit(solution)/shard_map/all_to_all | solution.py:290
  47.2 1.4 %shard_map.99 = (f32[64,512]{1,0:T(8,128)}, f32[64,512]{1,0:T(8,128)}, f32[64,512]{1,0:T(8,128)}) custom-call(bf16[32,24,128]{2,1,0:T(8,128)(2,1)S(1)} %all-to-all-done.incoming_ref, f32[64,512]{1,0:T(8,128)S(1)} %get-tuple-element.27.zt_ref, f32[64,512]{1,0:T(8,128)S(1)} %get-tuple-element.28.nt_ref), custom_call_target="tpu_custom_call" | custom-call | tf_op jit(solution)/shard_map/pallas_call | solution.py:291
  (1 shorter events, 0.0 us)
Async XLA Ops:
  2.5 14.8 %collective-permute-start = (bf16[512,128]{1,0:T(8,128)(2,1)}, bf16[512,128]{1,0:T(8,128)(2,1)S(1)}, u32[]{:S(2)}, u32[]{:S(2)}) collective-permute-start(bf16[512,128]{1,0:T(8,128)(2,1)} %shard_map.94.refs_1_.refs_3_), channel_id=1, source_target_pairs={{0,1},{1,0},{2,3},{3,2},{4,5},{5,4},{6,7},{7,6},{8,9},{9,8},{10,11... | collective-permute-start | bytes 393224 | tf_op jit(solution)/shard_map/ppermute | solution.py:225
  5.5 11.8 %collective-permute-start.1 = (bf16[512,128]{1,0:T(8,128)(2,1)}, bf16[512,128]{1,0:T(8,128)(2,1)S(1)}, u32[]{:S(2)}, u32[]{:S(2)}) collective-permute-start(bf16[512,128]{1,0:T(8,128)(2,1)} %shard_map.94.refs_1_.refs_3_), channel_id=1, source_target_pairs={{0,2},{1,3},{2,0},{3,1},{4,6},{5,7},{6,4},{7,5},{8,10},{9,11},{10,... | collective-permute-start | bytes 393224 | tf_op jit(solution)/shard_map/ppermute | solution.py:225
  7.0 10.2 %collective-permute-start.2 = (bf16[512,128]{1,0:T(8,128)(2,1)}, bf16[512,128]{1,0:T(8,128)(2,1)S(1)}, u32[]{:S(2)}, u32[]{:S(2)}) collective-permute-start(bf16[512,128]{1,0:T(8,128)(2,1)} %shard_map.94.refs_1_.refs_3_), channel_id=1, source_target_pairs={{0,3},{1,2},{2,1},{3,0},{4,7},{5,6},{6,5},{7,4},{8,11},{9,10},{10,... | collective-permute-start | bytes 393224 | tf_op jit(solution)/shard_map/ppermute | solution.py:225
  7.0 4.6 %collective-permute-start.3 = (s32[2,128]{1,0:T(2,128)}, s32[2,128]{1,0:T(2,128)S(1)}, u32[]{:S(2)}, u32[]{:S(2)}) collective-permute-start(s32[2,128]{1,0:T(2,128)} %bitcast.8), channel_id=1, source_target_pairs={{0,4},{1,5},{2,6},{3,7},{4,0},{5,1},{6,2},{7,3},{8,12},{9,13},{10,... | collective-permute-start | bytes 3080 | tf_op jit(solution)/shard_map/ppermute | solution.py:225
  9.1 5.8 %collective-permute-start.4 = (s32[2,128]{1,0:T(2,128)}, s32[2,128]{1,0:T(2,128)S(1)}, u32[]{:S(2)}, u32[]{:S(2)}) collective-permute-start(s32[2,128]{1,0:T(2,128)} %bitcast.9), channel_id=1, source_target_pairs={{0,8},{1,9},{2,10},{3,11},{4,12},{5,13},{6,14},{7,15},{8,0},{9,1},... | collective-permute-start | bytes 3080 | tf_op jit(solution)/shard_map/ppermute | solution.py:225
  11.7 5.6 %collective-permute-start.5 = (s32[2,128]{1,0:T(2,128)}, s32[2,128]{1,0:T(2,128)S(1)}, u32[]{:S(2)}, u32[]{:S(2)}) collective-permute-start(s32[2,128]{1,0:T(2,128)} %bitcast.10), channel_id=1, source_target_pairs={{0,12},{1,13},{2,14},{3,15},{4,8},{5,9},{6,10},{7,11},{8,4},{9,5},... | collective-permute-start | bytes 3080 | tf_op jit(solution)/shard_map/ppermute | solution.py:225
  17.2 0.9 %copy-start = (bf16[512,128]{1,0:T(8,128)(2,1)S(1)}, bf16[512,128]{1,0:T(8,128)(2,1)}, u32[]{:S(2)}) copy-start(bf16[512,128]{1,0:T(8,128)(2,1)} %shard_map.94.refs_1_.refs_3_) | copy-start | bytes 393220
  18.2 10.0 %slice-start = ((s8[8388608]{0:T(1024)(128)(4,1)}), s8[4194304]{0:T(1024)(128)(4,1)S(1)}, s32[]{:S(2)}) async-start(s8[8388608]{0:T(1024)(128)(4,1)} %bitcast.6), calls=%async_computation.1 | async-start | bytes 8388608
  18.8 7.2 %collective-permute-start.6 = (bf16[80,128]{1,0:T(8,128)(2,1)S(1)}, bf16[80,128]{1,0:T(8,128)(2,1)S(1)}, u32[]{:S(2)}, u32[]{:S(2)}) collective-permute-start(bf16[80,128]{1,0:T(8,128)(2,1)S(1)} %get-tuple-element.22), channel_id=1, source_target_pairs={{0,4},{1,5},{2,6},{3,7},{4,0},{5,1},{6,2},{7,3},{8,12},{9,13},{10,... | collective-permute-start | bytes 61448 | tf_op jit(solution)/shard_map/ppermute | solution.py:225
  18.9 7.1 %collective-permute-start.7 = (bf16[80,128]{1,0:T(8,128)(2,1)S(1)}, bf16[80,128]{1,0:T(8,128)(2,1)S(1)}, u32[]{:S(2)}, u32[]{:S(2)}) collective-permute-start(bf16[80,128]{1,0:T(8,128)(2,1)S(1)} %get-tuple-element.23), channel_id=1, source_target_pairs={{0,8},{1,9},{2,10},{3,11},{4,12},{5,13},{6,14},{7,15},{8,0},{9,1},... | collective-permute-start | bytes 61448 | tf_op jit(solution)/shard_map/ppermute | solution.py:225
  22.6 5.6 %collective-permute-start.8 = (bf16[80,128]{1,0:T(8,128)(2,1)S(1)}, bf16[80,128]{1,0:T(8,128)(2,1)S(1)}, u32[]{:S(2)}, u32[]{:S(2)}) collective-permute-start(bf16[80,128]{1,0:T(8,128)(2,1)S(1)} %get-tuple-element.24), channel_id=1, source_target_pairs={{0,12},{1,13},{2,14},{3,15},{4,8},{5,9},{6,10},{7,11},{8,4},{9,5},... | collective-permute-start | bytes 61448 | tf_op jit(solution)/shard_map/ppermute | solution.py:225
  23.2 0.7 %copy-start.5 = (s32[256]{0:T(256)S(1)}, s32[256]{0:T(256)}, u32[]{:S(2)}) copy-start(s32[256]{0:T(256)} %param.9) | copy-start | bytes 3076
  23.9 0.7 %copy-start.7 = (s32[256]{0:T(256)S(1)}, s32[256]{0:T(256)}, u32[]{:S(2)}) copy-start(s32[256]{0:T(256)} %param.10) | copy-start | bytes 3076
  24.6 0.9 %copy-start.1 = (bf16[512,128]{1,0:T(8,128)(2,1)S(1)}, bf16[512,128]{1,0:T(8,128)(2,1)}, u32[]{:S(2)}) copy-start(bf16[512,128]{1,0:T(8,128)(2,1)} %shard_map.94.refs_1_.refs_3_) | copy-start | bytes 393220
  24.6 0.9 %copy-start.6 = (s32[256]{0:T(256)S(1)}, s32[256]{0:T(256)}, u32[]{:S(2)}) copy-start(s32[256]{0:T(256)} %param.9) | copy-start | bytes 3076
  24.6 3.6 %slice-start.1 = ((s8[8388608]{0:T(1024)(128)(4,1)}), s8[4194304]{0:T(1024)(128)(4,1)S(1)}, s32[]{:S(2)}) async-start(s8[8388608]{0:T(1024)(128)(4,1)} %bitcast.6), calls=%async_computation.2 | async-start | bytes 8388608
  24.6 3.6 %copy-start.4 = (s32[8,128]{1,0:T(8,128)S(1)}, s32[8,128]{1,0:T(8,128)}, u32[]{:S(2)}) copy-start(s32[8,128]{1,0:T(8,128)} %labels_ref.1) | copy-start | bytes 12292
  25.5 11.9 %copy-start.2 = (f32[512,128]{1,0:T(8,128)S(1)}, f32[512,128]{1,0:T(8,128)}, u32[]{:S(2)}) copy-start(f32[512,128]{1,0:T(8,128)} %z_ref.1) | copy-start | bytes 786436
  25.5 11.9 %copy-start.3 = (f32[512,128]{1,0:T(8,128)S(1)}, f32[512,128]{1,0:T(8,128)}, u32[]{:S(2)}) copy-start(f32[512,128]{1,0:T(8,128)} %n_ref.1) | copy-start | bytes 786436
  33.3 13.9 %all-to-all-start = ((bf16[32,24,128]{2,1,0:T(8,128)(2,1)}), bf16[32,24,128]{2,1,0:T(8,128)(2,1)S(1)}, u32[]{:S(2)}, u32[]{:S(2)}) async-start(bf16[32,24,128]{2,1,0:T(8,128)(2,1)} %get-tuple-element.26), calls=%async_computation | async-start | bytes 393216 | tf_op jit(solution)/shard_map/all_to_all | solution.py:290

commit v3 on v1

v3 whole, which is shorter than its diff:
```python
import functools

import jax
import jax.numpy as jnp
from jax import lax
from jax.experimental import pallas as pl
from jax.experimental.pallas import tpu as pltpu
from jax.sharding import PartitionSpec as P

rate_alpha = 0.5
rate_beta = 1.0
lasso_weight = 0.5
ridge_weight = 1.0

f32, bf16, i32 = jnp.float32, jnp.bfloat16, jnp.int32
VMEM = pl.BlockSpec(memory_space=pltpu.VMEM)
SMEM = pl.BlockSpec(memory_space=pltpu.SMEM)


def shrink(z_acc, n_acc):
    soft = z_acc - jnp.clip(z_acc, -lasso_weight, lasso_weight)
    return -soft / ((rate_beta + jnp.sqrt(n_acc)) / rate_alpha + ridge_weight)


def iota(shape, dim):
    return lax.broadcasted_iota(i32, shape, dim)


def mask(hit):
    return hit.astype(f32).astype(bf16)


def before(size):
    return mask(iota((size, size), 0) < iota((size, size), 1))


def slot_ids(asked, cap, first, blk):
    tri = before(128)
    count = None
    picked = None
    for part in range(asked.shape[1]):
        local = asked[:, part, :] - first
        valid = (local >= 0) & (local < blk)
        ones = valid.astype(f32)
        rank = jnp.dot(ones.astype(bf16), tri, preferred_element_type=f32)
        total = jnp.sum(ones, axis=1, keepdims=True)
        if count is not None:
            rank = rank + count
            total = total + count
        count = total
        place = jnp.where(valid, rank.astype(i32), -1)[:, None, :]
        value = (local + 1).astype(f32)[:, None, :]
        shape = (place.shape[0], cap, 128)
        hit = jnp.broadcast_to(place, shape) == iota(shape, 1)
        here = jnp.where(hit, jnp.broadcast_to(value, shape), 0.0)
        picked = here if picked is None else picked + here
    return jnp.sum(picked, axis=2, keepdims=True).astype(i32) - 1


def one_hot_rows(ids, blk):
    rows, cap, _ = ids.shape
    shape = (rows, cap, blk)
    return mask(jnp.broadcast_to(ids, shape) == iota(shape, 2)).reshape(rows * cap, blk)


def prepare_kernel(
    shards, groups, cap, lines, block_ref, group_ref, z_ref, n_ref, pull_ref, order_ref, take_ref, put_ref, zt_ref, nt_ref
):
    blk, _ = z_ref.shape
    half = zt_ref.shape[0]
    tiles = block_ref.shape[1]
    rep = lax.axis_index("rep")
    pull_ref[...] = shrink(z_ref[...], n_ref[...]).astype(bf16)
    zt = z_ref[...].T
    nt = n_ref[...].T
    zt_ref[...] = jnp.where(rep == 0, zt[:half], zt[half:])
    nt_ref[...] = jnp.where(rep == 0, nt[:half], nt[half:])
    tri = before(tiles)
    owner = block_ref[...] // blk
    group = group_ref[...]

    def rank_in(key, count):
        same = jnp.broadcast_to(key, (count, tiles)) == iota((count, tiles), 0)
        rank = jnp.dot(mask(same), tri, preferred_element_type=f32)
        return jnp.sum(jnp.where(same, rank, 0.0), axis=0, keepdims=True)

    rank = rank_in(owner, shards)
    place = (group * (tiles // groups)).astype(f32) + rank_in(group, groups)
    move = (jnp.broadcast_to(place.astype(i32), (tiles, tiles)) == iota((tiles, tiles), 0)).astype(f32)
    slot = owner.astype(f32) * cap + rank
    column = jnp.sum(move * slot, axis=1, keepdims=True).astype(i32)
    take_ref[...] = mask(jnp.broadcast_to(column, (tiles, shards * cap)) == iota((tiles, shards * cap), 1))
    row = iota((8, tiles), 0)
    facts = jnp.where(
        row == 0,
        jnp.broadcast_to(owner.astype(f32), (8, tiles)),
        jnp.where(row == 1, jnp.broadcast_to(rank, (8, tiles)), iota((8, tiles), 1).astype(f32)),
    )
    facts = lax.dot_general(
        facts.astype(bf16), move.astype(bf16), (((1,), (1,)), ((), ())), preferred_element_type=f32
    )
    order_ref[...] = facts[2:3].astype(i32)
    owner = facts[0:1].astype(i32)
    rank = facts[1:2].astype(i32)
    at = iota((shards * lines, tiles), 0)
    left = jnp.where(rank < lines, owner * lines + rank, -1)
    right = jnp.where(rank >= lines, owner * lines + rank - lines, -1)
    put_ref[:, :tiles] = mask(jnp.broadcast_to(left, at.shape) == at)
    put_ref[:, tiles:] = mask(jnp.broadcast_to(right, at.shape) == at)


def answer_kernel(shards, cap, asked_ref, pull_ref, answer_ref):
    blk, lane = pull_ref.shape
    me = lax.axis_index("shard")
    rep = lax.axis_index("rep")
    asked = asked_ref[pl.ds(rep * shards, shards)]
    hot = one_hot_rows(slot_ids(asked, cap, me * blk, blk), blk)
    rows = jnp.dot(hot, pull_ref[...], preferred_element_type=f32)
    answer_ref[...] = rows.astype(bf16).reshape(shards, cap, lane)


def hot_kernel(blk, lines, after_ref, asked_ref, hot_ref):
    me = lax.axis_index("shard")
    ids = slot_ids(asked_ref[...], 2 * lines, me * blk, blk)
    hot_ref[0] = one_hot_rows(ids[:, :lines], blk)
    hot_ref[1] = one_hot_rows(ids[:, lines:], blk)


def worker_kernel(
    shards, cap, order_ref, answer_ref, take_ref, put_ref, labels_ref, tile_ref, margin_ref, out_ref, w_ref, sum_ref, grad_ref
):
    tiles, lane, _ = tile_ref.shape
    groups = labels_ref.shape[0]
    each = tiles // groups
    w_ref[...] = jnp.dot(take_ref[...], answer_ref[...].reshape(shards * cap, lane), preferred_element_type=f32)
    for g in range(groups):
        def add(j, acc):
            p = g * each + j
            return acc + tile_ref[order_ref[0, p]].astype(f32) * w_ref[pl.ds(p, 1), :]

        sum_ref[g] = lax.fori_loop(0, each, add, jnp.zeros((lane, lane), f32), unroll=8)
    margins = jnp.concatenate([jnp.sum(sum_ref[g], axis=1).reshape(1, lane) for g in range(groups)], axis=0)
    margin_ref[...] = margins
    resid = (jax.nn.sigmoid(margins) - labels_ref[...].astype(f32)).astype(bf16)
    for g in range(groups):
        row = resid[g : g + 1]
        wide = jnp.broadcast_to(row.astype(f32), (lane, lane)).T
        for j in range(0, each, 4):
            p = g * each + j
            pair = jnp.concatenate([tile_ref[order_ref[0, p]], tile_ref[order_ref[0, p + 1]]], axis=1)
            both = jnp.dot(row, pair, preferred_element_type=f32)
            grad_ref[p : p + 1, :] = both[:, :lane]
            grad_ref[p + 1 : p + 2, :] = both[:, lane:]
            for q in (p + 2, p + 3):
                grad_ref[q : q + 1, :] = jnp.sum(tile_ref[order_ref[0, q]].astype(f32) * wide, axis=0, keepdims=True)
    grads = grad_ref[...]
    half = lane // 2
    swapped = jnp.concatenate([grads[:, half:], grads[:, :half]], axis=1)
    left = iota((tiles, lane), 1) < half
    put = put_ref[...]
    for rep in range(2):
        first, second = (grads, swapped) if rep == 0 else (swapped, grads)
        sides = jnp.concatenate([jnp.where(left, first, 0.0), jnp.where(left, 0.0, second)], axis=0)
        sent = jnp.dot(put, sides.astype(bf16), preferred_element_type=f32).astype(bf16)
        out_ref[rep * shards : (rep + 1) * shards] = sent.reshape(shards, -1, lane)


def update_kernel(incoming_ref, hot_ref, zt_ref, nt_ref, z_out, n_out, w_out):
    sources, lines, lane = incoming_ref.shape
    half = lane // 2
    incoming = incoming_ref[...].reshape(sources * lines, lane)
    over_rows = (((0,), (0,)), ((), ()))
    left = lax.dot_general(incoming, hot_ref[0], over_rows, preferred_element_type=f32)
    right = lax.dot_general(incoming, hot_ref[1], over_rows, preferred_element_type=f32)
    total = left[:half] + right[half:]
    z_state = zt_ref[...]
    n_state = nt_ref[...]
    w_old = shrink(z_state, n_state)
    new_n = n_state + total * total
    sigma = (jnp.sqrt(new_n) - jnp.sqrt(n_state)) / rate_alpha
    new_z = z_state + total - sigma * w_old
    z_out[...] = new_z
    n_out[...] = new_n
    w_out[...] = shrink(new_z, new_n)


def call(kernel, out, specs, scratch=(), limit=16 << 20, flops=0):
    return pl.pallas_call(
        kernel,
        out_shape=out,
        in_specs=specs,
        out_specs=jax.tree.map(lambda _: VMEM, out),
        scratch_shapes=list(scratch),
        compiler_params=pltpu.CompilerParams(vmem_limit_bytes=limit),
        cost_estimate=pl.CostEstimate(flops=flops, bytes_accessed=0, transcendentals=0),
    )


def body(z_state, n_state, tile_values, tile_block, tile_group, labels):
    blk, lane = z_state.shape
    tiles = tile_block.shape[0]
    groups = labels.shape[0]
    shards = lax.axis_size("shard")
    reps = lax.axis_size("rep")
    half = lane // reps
    need = max(4, (tiles + shards - 2) // (shards - 1))
    cap = (need + 7) // 8 * 8
    lines = 8 if need <= 16 else (need + 31) // 32 * 16
    slots = shards * cap
    axes = ("rep", "shard")
    shape = jax.ShapeDtypeStruct

    raw = jnp.broadcast_to(tile_block.reshape(1, tiles // 128, 128), (reps * shards, tiles // 128, 128))
    asked = lax.all_to_all(raw, axes, split_axis=0, concat_axis=0, tiled=True)
    pull, order, take, put, zt, nt = call(
        functools.partial(prepare_kernel, shards, groups, cap, lines),
        (
            shape((blk, lane), bf16),
            shape((1, tiles), i32),
            shape((tiles, slots), bf16),
            shape((shards * lines, 2 * tiles), bf16),
            shape((half, blk), f32),
            shape((half, blk), f32),
        ),
        [VMEM] * 4,
        flops=4 * 10**9,
    )(tile_block.reshape(1, tiles), tile_group.reshape(1, tiles), z_state, n_state)
    answer = call(
        functools.partial(answer_kernel, shards, cap),
        shape((shards, cap, lane), bf16),
        [VMEM] * 2,
        flops=8 * 10**9,
    )(asked, pull)
    answer = lax.all_to_all(answer, "shard", split_axis=0, concat_axis=0, tiled=True)
    margins, outgoing = call(
        functools.partial(worker_kernel, shards, cap),
        (shape((groups, lane), f32), shape((reps * shards, lines, lane), bf16)),
        [SMEM] + [VMEM] * 5,
        [pltpu.VMEM((tiles, lane), f32), pltpu.VMEM((groups, lane, lane), f32), pltpu.VMEM((tiles, lane), f32)],
    )(order, answer, take, put, labels, tile_values)
    incoming = lax.all_to_all(outgoing, axes, split_axis=0, concat_axis=0, tiled=True)
    hot = call(
        functools.partial(hot_kernel, blk, lines), shape((2, reps * shards * lines, blk), bf16), [VMEM] * 2, flops=4 * 10**9
    )(margins, asked)
    outs = call(update_kernel, (shape((half, blk), f32),) * 3, [VMEM] * 4)(incoming, hot, zt, nt)
    return (margins,) + tuple(o.T for o in outs)


def solution(mesh):
    placed = (
        P("shard", None),
        P("shard", None),
        P(("rep", "shard"), None, None),
        P(("rep", "shard")),
        P(("rep", "shard")),
        P(("rep", "shard"), None),
    )
    return jax.shard_map(
        body,
        mesh=mesh,
        in_specs=placed,
        out_specs=(
            P(("rep", "shard"), None),
            P("shard", "rep"),
            P("shard", "rep"),
            P("shard", "rep"),
        ),
        check_vma=False,
    )
```

time: 51.3 us -> 45.4 us (0.88)
  starting transfers between devices: 6.08 us -> 9.87 us
  local copies, waits for them, and re-layouts: 8.98 us -> 5.25 us
  blocking collectives: 14.3 us -> 11.2 us
  waiting for transfers between devices: 12.9 us -> 10 us
    unnamed x18 -> x14, local copies, waits for them, and re-layouts: 8.29 us -> 3.94 us
    all_to_all x1, starting transfers between devices: 3.51 us -> 7.3 us  [body(): asked = lax.all_to_all(raw, axes, split_axis=0, concat_axis=0, tiled=True)]
    all_to_all x1, blocking collectives: 14.3 us -> 11.2 us  [body(): lax.all_to_all(answer, 'shard', split_axis=0, concat_axis=0, tiled=True)]
    all_to_all x1, waiting for transfers between devices: 5.81 us -> 3.37 us  [body(): asked = lax.all_to_all(raw, axes, split_axis=0, concat_axis=0, tiled=True)]
    pallas_call x1, Pallas kernels: 1.21 us -> 0.52 us  [body(): call(functools.partial(answer_kernel, shards, cap), shape((shards, cap, l...]
    pallas_call x1, Pallas kernels: 4.51 us -> 5.15 us  [body(): call(functools.partial(worker_kernel, shards, cap), (shape((groups, lane)...]
    broadcast_in_dim x1, local copies, waits for them, and re-layouts: 0.69 us -> 1.3 us  [body(): jnp.broadcast_to(tile_block.reshape(1, tiles // 128, 128), (reps * shards...]
  transfers between devices with their start and end apart: 2 -> 2, of which waited for: 2 -> 2; matrix products, arithmetic and copies ran while one was open for 0% -> 0% of each run, Pallas kernels for 2% -> 3%
where the time goes in v3:
time: 45.4 us; the launch traced here: 45 us
  blocking collectives  11.2 us (25%)
  waiting for transfers between devices  10 us (22%)
  starting transfers between devices  9.87 us (22%)
  Pallas kernels  7.98 us (18%)
  local copies, waits for them, and re-layouts  5.25 us (12%)
  between operations  0.69 us (2%)
    all_to_all x1, blocking collectives, body(): lax.all_to_all(answer, 'shard', split_axis=0, concat_axis=0, tiled=True)  11.2 us
    all_to_all x1, starting transfers between devices, body(): asked = lax.all_to_all(raw, axes, split_axis=0, concat_axis=0, tiled=True)  7.3 us
    all_to_all x1, waiting for transfers between devices, body(): lax.all_to_all(outgoing, axes, split_axis=0, concat_axis=0, tiled=True)  6.63 us
    pallas_call x1, Pallas kernels, body(): call(functools.partial(worker_kernel, shards, cap), (shape((groups, lane)...  5.15 us
    unnamed x14, local copies, waits for them, and re-layouts  3.94 us
    all_to_all x1, waiting for transfers between devices, body(): asked = lax.all_to_all(raw, axes, split_axis=0, concat_axis=0, tiled=True)  3.37 us
    all_to_all x1, starting transfers between devices, body(): lax.all_to_all(outgoing, axes, split_axis=0, concat_axis=0, tiled=True)  2.58 us
    broadcast_in_dim x1, local copies, waits for them, and re-layouts, body(): jnp.broadcast_to(tile_block.reshape(1, tiles // 128, 128), (reps * shards...  1.3 us
  transfers between devices with their start and end apart: 2, of which 2 were waited for; matrix products, arithmetic and copies ran while one was open for 0% of the time, Pallas kernels for 3%

profile of v3, /device:TPU:0, one launch (start us, length us, event | category | flops | bytes accessed | tf_op | source)
XLA Modules:
  0.0 45.0 jit_solution(2230008290000943301)
XLA Ops:
  0.6 1.3 %broadcast_in_dim.8 = s32[32,2,128]{2,1,0:T(2,128)} broadcast(s32[2,128]{1,0:T(2,128)} %bitcast.6), dimensions={1,2} | broadcast | bytes 33792 | tf_op jit(solution)/shard_map/broadcast_in_dim | solution.py:213
  1.9 7.3 %all-to-all-start = ((s32[32,2,128]{2,1,0:T(2,128)}), s32[32,2,128]{2,1,0:T(2,128)S(1)}, u32[]{:S(2)}, u32[]{:S(2)}) async-start(s32[32,2,128]{2,1,0:T(2,128)} %broadcast_in_dim.8), calls=%async_computation | async-start | bytes 65536 | tf_op jit(solution)/shard_map/all_to_all | solution.py:214
  9.2 0.0 copy-start.2
  9.3 0.7 %copy-done.2 = s32[256]{0:T(256)S(1)} copy-done((s32[256]{0:T(256)S(1)}, s32[256]{0:T(256)}, u32[]{:S(2)}) %copy-start.2) | copy-done | bytes 1048
  9.9 0.0 copy-start.3
  9.9 0.9 %copy-done.3 = f32[512,128]{1,0:T(8,128)S(1)} copy-done((f32[512,128]{1,0:T(8,128)S(1)}, f32[512,128]{1,0:T(8,128)}, u32[]{:S(2)}) %copy-start.3) | copy-done | bytes 262168
  10.9 0.0 copy-start.4
  10.9 0.9 %copy-done.4 = f32[512,128]{1,0:T(8,128)S(1)} copy-done((f32[512,128]{1,0:T(8,128)S(1)}, f32[512,128]{1,0:T(8,128)}, u32[]{:S(2)}) %copy-start.4) | copy-done | bytes 262168
  11.8 0.0 copy-start.6
  11.8 0.7 %copy-done.6 = s32[256]{0:T(256)S(1)} copy-done((s32[256]{0:T(256)S(1)}, s32[256]{0:T(256)}, u32[]{:S(2)}) %copy-start.6) | copy-done | bytes 1048
  12.5 0.6 %shard_map.93 = (bf16[512,128]{1,0:T(8,128)(2,1)S(1)}, s32[1,256]{1,0:T(1,128)S(1)}, bf16[256,384]{1,0:T(8,128)(2,1)S(1)}, bf16[256,512]{1,0:T(8,128)(2,1)S(1)},...) custom-call(s32[1,256]{1,0:T(1,128)S(1)} %bitcast.7, s32[1,256]{1,0:T(1,128)S(1)} %bitcast.8, f32[512,128]{1,0:T(8,128)S(1)} %copy-done.3, ...), custom_call_target="tpu_custom_call" | custom-call | flops 4000000000 | tf_op jit(solution)/shard_map/pallas_call | solution.py:215
  13.1 3.4 %all-to-all-done.asked_ref = s32[32,2,128]{2,1,0:T(2,128)S(1)} async-done(((s32[32,2,128]{2,1,0:T(2,128)}), s32[32,2,128]{2,1,0:T(2,128)S(1)}, u32[]{:S(2)}, u32[]{:S(2)}) %all-to-all-start) | async-done | bytes 32800 | tf_op jit(solution)/shard_map/all_to_all | solution.py:214
  16.4 0.0 copy-start
  16.4 0.0 copy-start.1
  16.4 0.5 %shard_map.94 = bf16[16,24,128]{2,1,0:T(8,128)(2,1)S(1)} custom-call(s32[32,2,128]{2,1,0:T(2,128)S(1)} %all-to-all-done.asked_ref, bf16[512,128]{1,0:T(8,128)(2,1)S(1)} %get-tuple-element.16.pull_ref), custom_call_target="tpu_custom_call" | custom-call | flops 8000000000 | tf_op jit(solution)/shard_map/pallas_call | solution.py:228
  17.0 11.2 %all_to_all.15.answer_ref = bf16[16,24,128]{2,1,0:T(8,128)(2,1)S(1)} all-to-all(bf16[16,24,128]{2,1,0:T(8,128)(2,1)S(1)} %shard_map.94), channel_id=1, replica_groups=mesh['rep'=2,'shard'=16] {'shard'}, dimensions={0} | all-to-all | bytes 196608 | tf_op jit(solution)/shard_map/all_to_all | solution.py:234
  28.2 0.0 copy-done
  28.2 0.0 copy-done.1
  28.2 5.2 %shard_map.95 = (f32[8,128]{1,0:T(8,128)}, bf16[32,16,128]{2,1,0:T(8,128)(2,1)}) custom-call(s32[1,256]{1,0:T(1,128)S(1)} %get-tuple-element.15.order_ref, bf16[16,24,128]{2,1,0:T(8,128)(2,1)S(1)} %all_to_all.15.answer_ref, bf16[256,384]{1,0:T(8,128)(2,1)S(1)} %get-tuple-element.17.take_ref, bf16[256,512]{1,0:T(8,128)(2,1)S(1)} %get-tuple-element.18.put_ref, ...), custom_call_target="tpu_custom_call" | custom-call | tf_op jit(solution)/shard_map/pallas_call | solution.py:235
  33.4 2.6 %all-to-all-start.2 = ((bf16[32,16,128]{2,1,0:T(8,128)(2,1)}), bf16[32,16,128]{2,1,0:T(8,128)(2,1)S(1)}, u32[]{:S(2)}, u32[]{:S(2)}) async-start(bf16[32,16,128]{2,1,0:T(8,128)(2,1)} %get-tuple-element.20), calls=%async_computation.2 | async-start | bytes 262144 | tf_op jit(solution)/shard_map/all_to_all | solution.py:241
  36.0 0.0 copy-start.5
  36.0 0.7 %copy-done.5 = f32[8,128]{1,0:T(8,128)S(1)} copy-done((f32[8,128]{1,0:T(8,128)S(1)}, f32[8,128]{1,0:T(8,128)}, u32[]{:S(2)}) %copy-start.5) | copy-done | bytes 4120
  36.7 0.6 %shard_map.96.hot_ref = bf16[2,512,512]{2,1,0:T(8,128)(2,1)S(1)} custom-call(f32[8,128]{1,0:T(8,128)S(1)} %copy-done.5, s32[32,2,128]{2,1,0:T(2,128)S(1)} %all-to-all-done.asked_ref), custom_call_target="tpu_custom_call" | custom-call | flops 4000000000 | tf_op jit(solution)/shard_map/pallas_call | solution.py:242
  37.2 6.6 %all-to-all-done.2.incoming_ref = bf16[32,16,128]{2,1,0:T(8,128)(2,1)S(1)} async-done(((bf16[32,16,128]{2,1,0:T(8,128)(2,1)}), bf16[32,16,128]{2,1,0:T(8,128)(2,1)S(1)}, u32[]{:S(2)}, u32[]{:S(2)}) %all-to-all-start.2) | async-done | bytes 131104 | tf_op jit(solution)/shard_map/all_to_all | solution.py:241
  43.9 1.2 %shard_map.97 = (f32[64,512]{1,0:T(8,128)}, f32[64,512]{1,0:T(8,128)}, f32[64,512]{1,0:T(8,128)}) custom-call(bf16[32,16,128]{2,1,0:T(8,128)(2,1)S(1)} %all-to-all-done.2.incoming_ref, bf16[2,512,512]{2,1,0:T(8,128)(2,1)S(1)} %shard_map.96.hot_ref, f32[64,512]{1,0:T(8,128)S(1)} %get-tuple-element.21.zt_ref, f32[64,512]{1,0:T(8,128)S(1)} %get-tuple-element.22.nt_ref), custom_call_target="tpu_custom_call" | custom-call | tf_op jit(solution)/shard_map/pallas_call | solution.py:245
Async XLA Ops:
  1.9 14.5 %all-to-all-start = ((s32[32,2,128]{2,1,0:T(2,128)}), s32[32,2,128]{2,1,0:T(2,128)S(1)}, u32[]{:S(2)}, u32[]{:S(2)}) async-start(s32[32,2,128]{2,1,0:T(2,128)} %broadcast_in_dim.8), calls=%async_computation | async-start | bytes 65536 | tf_op jit(solution)/shard_map/all_to_all | solution.py:214
  9.2 0.7 %copy-start.2 = (s32[256]{0:T(256)S(1)}, s32[256]{0:T(256)}, u32[]{:S(2)}) copy-start(s32[256]{0:T(256)} %param.9) | copy-start | bytes 3076
  9.9 0.9 %copy-start.3 = (f32[512,128]{1,0:T(8,128)S(1)}, f32[512,128]{1,0:T(8,128)}, u32[]{:S(2)}) copy-start(f32[512,128]{1,0:T(8,128)} %z_ref.1) | copy-start | bytes 786436
  10.9 0.9 %copy-start.4 = (f32[512,128]{1,0:T(8,128)S(1)}, f32[512,128]{1,0:T(8,128)}, u32[]{:S(2)}) copy-start(f32[512,128]{1,0:T(8,128)} %n_ref.1) | copy-start | bytes 786436
  11.8 0.7 %copy-start.6 = (s32[256]{0:T(256)S(1)}, s32[256]{0:T(256)}, u32[]{:S(2)}) copy-start(s32[256]{0:T(256)} %param.10) | copy-start | bytes 3076
  16.4 11.8 %copy-start = (bf16[256,128,128]{2,1,0:T(8,128)(2,1)S(1)}, bf16[256,128,128]{2,1,0:T(8,128)(2,1)}, u32[]{:S(2)}) copy-start(bf16[256,128,128]{2,1,0:T(8,128)(2,1)} %tile_ref.1) | copy-start | bytes 25165828
  16.4 11.8 %copy-start.1 = (s32[8,128]{1,0:T(8,128)S(1)}, s32[8,128]{1,0:T(8,128)}, u32[]{:S(2)}) copy-start(s32[8,128]{1,0:T(8,128)} %labels_ref.1) | copy-start | bytes 12292
  33.4 10.5 %all-to-all-start.2 = ((bf16[32,16,128]{2,1,0:T(8,128)(2,1)}), bf16[32,16,128]{2,1,0:T(8,128)(2,1)S(1)}, u32[]{:S(2)}, u32[]{:S(2)}) async-start(bf16[32,16,128]{2,1,0:T(8,128)(2,1)} %get-tuple-element.20), calls=%async_computation.2 | async-start | bytes 262144 | tf_op jit(solution)/shard_map/all_to_all | solution.py:241
  36.0 0.7 %copy-start.5 = (f32[8,128]{1,0:T(8,128)S(1)}, f32[8,128]{1,0:T(8,128)}, u32[]{:S(2)}) copy-start(f32[8,128]{1,0:T(8,128)} %get-tuple-element.11.after_ref) | copy-start | bytes 12292

commit v4 on v3

v4 whole, which is shorter than its diff:
```python
import functools

import jax
import jax.numpy as jnp
from jax import lax
from jax.experimental import pallas as pl
from jax.experimental.pallas import tpu as pltpu
from jax.sharding import PartitionSpec as P

rate_alpha = 0.5
rate_beta = 1.0
lasso_weight = 0.5
ridge_weight = 1.0

f32, bf16, i32 = jnp.float32, jnp.bfloat16, jnp.int32
VMEM = pl.BlockSpec(memory_space=pltpu.VMEM)
SMEM = pl.BlockSpec(memory_space=pltpu.SMEM)
HBM = pl.BlockSpec(memory_space=pltpu.HBM)


def shrink(z_acc, n_acc):
    soft = z_acc - jnp.clip(z_acc, -lasso_weight, lasso_weight)
    return -soft / ((rate_beta + jnp.sqrt(n_acc)) / rate_alpha + ridge_weight)


def iota(shape, dim):
    return lax.broadcasted_iota(i32, shape, dim)


def mask(hit):
    return hit.astype(f32).astype(bf16)


def before(size):
    return mask(iota((size, size), 0) < iota((size, size), 1))


def asked_slots(asked, first, blk):
    tri = before(128)
    count = 0.0
    ranks = []
    locals_ = []
    for part in range(asked.shape[1]):
        local = asked[:, part, :] - first
        valid = (local >= 0) & (local < blk)
        ones = valid.astype(f32)
        rank = jnp.dot(ones.astype(bf16), tri, preferred_element_type=f32) + count
        count = count + jnp.sum(ones, axis=1, keepdims=True)
        ranks.append(jnp.where(valid, rank, -1.0))
        locals_.append(jnp.where(valid, local, 0))
    return jnp.concatenate(ranks, axis=1), jnp.concatenate(locals_, axis=1)


def slot_rows(rank, local, lines, *firsts):
    workers, tiles = rank.shape
    rows = workers * lines
    row = iota((rows, workers), 0)
    worker = iota((rows, workers), 1) * lines
    spread = mask((row >= worker) & (row < worker + lines))
    line = (iota((rows, tiles), 0) % lines).astype(f32)
    number = local + 1
    high = number // 256
    low = number - high * 256
    each_rank = jnp.dot(spread, rank.astype(bf16), preferred_element_type=f32)
    each_high = jnp.dot(spread, high.astype(f32).astype(bf16), preferred_element_type=f32)
    each_low = jnp.dot(spread, low.astype(f32).astype(bf16), preferred_element_type=f32)
    each = each_high * 256.0 + each_low
    columns = []
    for first in firsts:
        picked = jnp.where(each_rank - first == line, each, 0.0)
        columns.append(jnp.sum(picked, axis=1, keepdims=True).astype(i32) - 1)
    return columns


def one_hot(column, blk):
    shape = (column.shape[0], blk)
    return mask(jnp.broadcast_to(column, shape) == iota(shape, 1))


def prepare_kernel(
    shards, groups, lines, block_hbm, group_hbm, z_hbm, n_hbm, pull_ref, order_ref, take_ref, put_ref, zt_ref, nt_ref,
    block_ref, group_ref, z_ref, n_ref, sem
):
    copies = [
        pltpu.make_async_copy(source, target, sem.at[i])
        for i, (source, target) in enumerate(
            [(block_hbm, block_ref), (group_hbm, group_ref), (z_hbm, z_ref), (n_hbm, n_ref)]
        )
    ]
    for copy in copies:
        copy.start()
    copies[0].wait()
    copies[1].wait()
    blk, _ = z_ref.shape
    half = zt_ref.shape[0]
    parts = block_ref.shape[0]
    tiles = parts * 128
    rep = lax.axis_index("rep")
    tri = before(tiles)
    owner = jnp.concatenate([block_ref[i : i + 1] for i in range(parts)], axis=1) // blk
    group = jnp.concatenate([group_ref[i : i + 1] for i in range(parts)], axis=1)

    def rank_in(key, count):
        same = jnp.broadcast_to(key, (count, tiles)) == iota((count, tiles), 0)
        rank = jnp.dot(mask(same), tri, preferred_element_type=f32)
        return jnp.sum(jnp.where(same, rank, 0.0), axis=0, keepdims=True)

    rank = rank_in(owner, shards)
    place = (group * (tiles // groups)).astype(f32) + rank_in(group, groups)
    move = (jnp.broadcast_to(place.astype(i32), (tiles, tiles)) == iota((tiles, tiles), 0)).astype(f32)
    late = rank >= lines
    slot = owner.astype(f32) * lines + rank + jnp.where(late, (shards - 1) * lines * 1.0, 0.0)
    column = jnp.sum(move * slot, axis=1, keepdims=True).astype(i32)
    take_ref[...] = mask(jnp.broadcast_to(column, take_ref.shape) == iota(take_ref.shape, 1))
    row = iota((8, tiles), 0)
    facts = jnp.where(
        row == 0,
        jnp.broadcast_to(owner.astype(f32), (8, tiles)),
        jnp.where(row == 1, jnp.broadcast_to(rank, (8, tiles)), iota((8, tiles), 1).astype(f32)),
    )
    facts = lax.dot_general(
        facts.astype(bf16), move.astype(bf16), (((1,), (1,)), ((), ())), preferred_element_type=f32
    )
    order_ref[...] = facts[2:3].astype(i32)
    owner = facts[0:1].astype(i32)
    rank = facts[1:2].astype(i32)
    at = iota((shards * lines, tiles), 0)
    left = jnp.where(rank < lines, owner * lines + rank, -1)
    right = jnp.where(rank >= lines, owner * lines + rank - lines, -1)
    put_ref[:, :tiles] = mask(jnp.broadcast_to(left, at.shape) == at)
    put_ref[:, tiles:] = mask(jnp.broadcast_to(right, at.shape) == at)
    copies[2].wait()
    copies[3].wait()
    pull_ref[...] = shrink(z_ref[...], n_ref[...]).astype(bf16)
    zt = z_ref[...].T
    nt = n_ref[...].T
    zt_ref[...] = jnp.where(rep == 0, zt[:half], zt[half:])
    nt_ref[...] = jnp.where(rep == 0, nt[:half], nt[half:])


def answer_kernel(lines, asked_ref, pull_ref, answer_ref):
    blk, lane = pull_ref.shape
    me = lax.axis_index("shard")
    rep = lax.axis_index("rep")
    rank, local = asked_slots(asked_ref[...], me * blk, blk)
    (column,) = slot_rows(rank, local, lines, (rep * lines).astype(f32))
    answer_ref[...] = jnp.dot(one_hot(column, blk), pull_ref[...], preferred_element_type=f32).astype(bf16)


def worker_kernel(
    lines, order_ref, answer_ref, take_ref, put_ref, labels_ref, asked_ref, tile_ref, margin_ref, out_ref, hot_ref,
    w_ref, sum_ref, grad_ref
):
    tiles, lane, _ = tile_ref.shape
    groups = labels_ref.shape[0]
    each = tiles // groups
    w_ref[...] = jnp.dot(take_ref[...], answer_ref[...], preferred_element_type=f32)
    for g in range(groups):
        def add(j, acc):
            p = g * each + j
            return acc + tile_ref[order_ref[0, p]].astype(f32) * w_ref[pl.ds(p, 1), :]

        sum_ref[g] = lax.fori_loop(0, each, add, jnp.zeros((lane, lane), f32), unroll=8)
    margins = jnp.concatenate([jnp.sum(sum_ref[g], axis=1).reshape(1, lane) for g in range(groups)], axis=0)
    margin_ref[...] = margins
    resid = (jax.nn.sigmoid(margins) - labels_ref[...].astype(f32)).astype(bf16)
    rows, blk = hot_ref.shape[1:]
    share = rows // groups
    rank, local = asked_slots(asked_ref[...], lax.axis_index("shard") * blk, blk)
    columns = slot_rows(rank, local, lines, 0.0, float(lines))
    for g in range(groups):
        for side, column in enumerate(columns):
            hot_ref[side, g * share : (g + 1) * share] = one_hot(column[g * share : (g + 1) * share], blk)
        row = resid[g : g + 1]
        for j in range(0, each, 2):
            p = g * each + j
            pair = jnp.concatenate([tile_ref[order_ref[0, p]], tile_ref[order_ref[0, p + 1]]], axis=1)
            both = jnp.dot(row, pair, preferred_element_type=f32)
            grad_ref[p : p + 1, :] = both[:, :lane]
            grad_ref[p + 1 : p + 2, :] = both[:, lane:]
    grads = grad_ref[...]
    half = lane // 2
    swapped = jnp.concatenate([grads[:, half:], grads[:, :half]], axis=1)
    left = iota((tiles, lane), 1) < half
    put = put_ref[...]
    for rep in range(2):
        first, second = (grads, swapped) if rep == 0 else (swapped, grads)
        sides = jnp.concatenate([jnp.where(left, first, 0.0), jnp.where(left, 0.0, second)], axis=0)
        sent = jnp.dot(put, sides.astype(bf16), preferred_element_type=f32).astype(bf16)
        out_ref[rep * sent.shape[0] : (rep + 1) * sent.shape[0]] = sent


def update_kernel(incoming_ref, hot_ref, zt_ref, nt_ref, z_out, n_out, w_out):
    half = zt_ref.shape[0]
    incoming = incoming_ref[...]
    over_rows = (((0,), (0,)), ((), ()))
    left = lax.dot_general(incoming, hot_ref[0], over_rows, preferred_element_type=f32)
    right = lax.dot_general(incoming, hot_ref[1], over_rows, preferred_element_type=f32)
    total = left[:half] + right[half:]
    z_state = zt_ref[...]
    n_state = nt_ref[...]
    w_old = shrink(z_state, n_state)
    new_n = n_state + total * total
    sigma = (jnp.sqrt(new_n) - jnp.sqrt(n_state)) / rate_alpha
    new_z = z_state + total - sigma * w_old
    z_out[...] = new_z
    n_out[...] = new_n
    w_out[...] = shrink(new_z, new_n)


def call(kernel, out, specs, scratch=(), limit=16 << 20, flops=0):
    return pl.pallas_call(
        kernel,
        out_shape=out,
        in_specs=specs,
        out_specs=jax.tree.map(lambda _: VMEM, out),
        scratch_shapes=list(scratch),
        compiler_params=pltpu.CompilerParams(vmem_limit_bytes=limit),
        cost_estimate=pl.CostEstimate(flops=flops, bytes_accessed=0, transcendentals=0),
    )


def body(z_state, n_state, tile_values, tile_block, tile_group, labels):
    blk, lane = z_state.shape
    tiles = tile_block.shape[0]
    groups = labels.shape[0]
    shards = lax.axis_size("shard")
    reps = lax.axis_size("rep")
    half = lane // reps
    need = max(4, (tiles + shards - 2) // (shards - 1))
    lines = (need + 3) // 4 * 2
    devices = reps * shards
    parts = tiles // 128
    shape = jax.ShapeDtypeStruct
    in_hbm = functools.partial(pltpu.with_memory_space_constraint, memory_space=pltpu.HBM)

    def swap(x):
        return lax.all_to_all(x, ("rep", "shard"), split_axis=0, concat_axis=0, tiled=True)

    def swap_rows(x):
        return swap(x.reshape(devices, lines // 2, 2, lane)).reshape(x.shape)

    ids = tile_block.reshape(parts, 128)
    asked = swap(jnp.broadcast_to(ids[None], (devices, parts, 128)))
    pull, order, take, put, zt, nt = call(
        functools.partial(prepare_kernel, shards, groups, lines),
        (
            shape((blk, lane), bf16),
            shape((1, tiles), i32),
            shape((tiles, devices * lines), bf16),
            shape((shards * lines, 2 * tiles), bf16),
            shape((half, blk), f32),
            shape((half, blk), f32),
        ),
        [HBM] * 4,
        [pltpu.VMEM((parts, 128), i32)] * 2 + [pltpu.VMEM((blk, lane), f32)] * 2 + [pltpu.SemaphoreType.DMA((4,))],
        flops=4 * 10**9,
    )(*(in_hbm(x) for x in (ids, tile_group.reshape(parts, 128), z_state, n_state)))
    answer = call(
        functools.partial(answer_kernel, lines),
        shape((devices * lines, lane), bf16),
        [VMEM] * 2,
        flops=8 * 10**9,
    )(asked, pull)
    margins, outgoing, hot = call(
        functools.partial(worker_kernel, lines),
        (
            shape((groups, lane), f32),
            shape((devices * lines, lane), bf16),
            shape((2, devices * lines, blk), bf16),
        ),
        [SMEM] + [VMEM] * 6,
        [pltpu.VMEM((tiles, lane), f32), pltpu.VMEM((groups, lane, lane), f32), pltpu.VMEM((tiles, lane), f32)],
    )(order, swap_rows(answer), take, put, labels, asked, tile_values)
    incoming = swap_rows(outgoing)
    outs = call(update_kernel, (shape((half, blk), f32),) * 3, [VMEM] * 4)(incoming, hot, zt, nt)
    return (margins,) + tuple(o.T for o in outs)


def solution(mesh):
    placed = (
        P("shard", None),
        P("shard", None),
        P(("rep", "shard"), None, None),
        P(("rep", "shard")),
        P(("rep", "shard")),
        P(("rep", "shard"), None),
    )
    return jax.shard_map(
        body,
        mesh=mesh,
        in_specs=placed,
        out_specs=(
            P(("rep", "shard"), None),
            P("shard", "rep"),
            P("shard", "rep"),
            P("shard", "rep"),
        ),
        check_vma=False,
    )
```

time: 45.4 us -> 42 us (0.925)
  blocking collectives: 11.2 us -> 18.6 us
  waiting for transfers between devices: 10 us -> 5.75 us
  local copies, waits for them, and re-layouts: 5.25 us -> 1.31 us
  starting transfers between devices: 9.87 us -> 7.3 us
    all_to_all x1 -> x2, blocking collectives: 11.2 us -> 18.6 us  [swap(): lax.all_to_all(x, ('rep', 'shard'), split_axis=0, concat_axis=0, tiled=True)]
    all_to_all x2 -> x1, waiting for transfers between devices: 10 us -> 5.75 us  [swap(): lax.all_to_all(x, ('rep', 'shard'), split_axis=0, concat_axis=0, tiled=True)]
    unnamed x14 -> x4, local copies, waits for them, and re-layouts: 3.94 us -> 0.01 us
    all_to_all x2 -> x1, starting transfers between devices: 9.87 us -> 7.3 us  [swap(): lax.all_to_all(x, ('rep', 'shard'), split_axis=0, concat_axis=0, tiled=True)]
    pallas_call x4 -> x3, Pallas kernels: 6.83 us -> 6.97 us  [the longest x1 4.69 us: body(): call(functools.partial(worker_kernel, lines), (shape((groups, lane), f32)...]
  transfers between devices with their start and end apart: 2 -> 1, of which waited for: 2 -> 1; matrix products, arithmetic and copies ran while one was open for 0% -> 0% of each run, Pallas kernels for 3% -> 3%
where the time goes in v4:
time: 42 us; the launch traced here: 41.8 us
  blocking collectives  18.6 us (44%)
  Pallas kernels  8.12 us (19%)
  starting transfers between devices  7.3 us (17%)
  waiting for transfers between devices  5.75 us (14%)
  local copies, waits for them, and re-layouts  1.31 us (3%)
  between operations  0.66 us (2%)
    all_to_all x2, blocking collectives, swap(): lax.all_to_all(x, ('rep', 'shard'), split_axis=0, concat_axis=0, tiled=True)  18.6 us
    all_to_all x1, starting transfers between devices, swap(): lax.all_to_all(x, ('rep', 'shard'), split_axis=0, concat_axis=0, tiled=True)  7.3 us
    all_to_all x1, waiting for transfers between devices, swap(): lax.all_to_all(x, ('rep', 'shard'), split_axis=0, concat_axis=0, tiled=True)  5.75 us
    pallas_call x1, Pallas kernels, body(): call(functools.partial(worker_kernel, lines), (shape((groups, lane), f32)...  4.69 us
    pallas_call x1, Pallas kernels, body(): call(functools.partial(prepare_kernel, shards, groups, lines), (shape((bl...  1.44 us
    broadcast_in_dim x1, local copies, waits for them, and re-layouts, body(): asked = swap(jnp.broadcast_to(ids[None], (devices, parts, 128)))  1.3 us
    pallas_call x1, Pallas kernels, body(): call(update_kernel, (shape((half, blk), f32),) * 3, [VMEM] * 4)  1.15 us
  transfers between devices with their start and end apart: 1, of which 1 were waited for; matrix products, arithmetic and copies ran while one was open for 0% of the time, Pallas kernels for 3%

profile of v4, /device:TPU:0, one launch (start us, length us, event | category | flops | bytes accessed | tf_op | source)
XLA Modules:
  0.0 41.8 jit_solution(17674851853654531629)
XLA Ops:
  0.6 1.3 %broadcast_in_dim.2 = s32[32,2,128]{2,1,0:T(2,128)} broadcast(s32[2,128]{1,0:T(2,128)} %bitcast.13), dimensions={1,2} | broadcast | bytes 33792 | tf_op jit(solution)/shard_map/broadcast_in_dim | solution.py:244
  1.9 7.3 %all-to-all-start = ((s32[32,2,128]{2,1,0:T(2,128)}), s32[32,2,128]{2,1,0:T(2,128)S(1)}, u32[]{:S(2)}, u32[]{:S(2)}) async-start(s32[32,2,128]{2,1,0:T(2,128)} %broadcast_in_dim.2), calls=%async_computation | async-start | bytes 65536 | tf_op jit(solution)/shard_map/all_to_all | solution.py:238
  9.2 1.4 %shard_map.93 = (bf16[512,128]{1,0:T(8,128)(2,1)S(1)}, s32[1,256]{1,0:T(1,128)S(1)}, bf16[256,320]{1,0:T(8,128)(2,1)S(1)}, bf16[160,512]{1,0:T(8,128)(2,1)S(1)},...) custom-call(s32[2,128]{1,0:T(2,128)} %bitcast.14, s32[2,128]{1,0:T(2,128)} %bitcast.18, f32[512,128]{1,0:T(8,128)} %z_hbm.1, ...), custom_call_target="tpu_custom_call" | custom-call | flops 4000000000 | tf_op jit(solution)/shard_map/pallas_call | solution.py:245
  10.7 5.8 %all-to-all-done.asked_ref = s32[32,2,128]{2,1,0:T(2,128)S(1)} async-done(((s32[32,2,128]{2,1,0:T(2,128)}), s32[32,2,128]{2,1,0:T(2,128)S(1)}, u32[]{:S(2)}, u32[]{:S(2)}) %all-to-all-start) | async-done | bytes 32800 | tf_op jit(solution)/shard_map/all_to_all | solution.py:238
  16.4 0.0 copy-start
  16.4 0.0 copy-start.1
  16.4 0.8 %shard_map.94 = bf16[320,128]{1,0:T(8,128)(2,1)S(1)} custom-call(s32[32,2,128]{2,1,0:T(2,128)S(1)} %all-to-all-done.asked_ref, bf16[512,128]{1,0:T(8,128)(2,1)S(1)} %get-tuple-element.17.pull_ref), custom_call_target="tpu_custom_call" | custom-call | flops 8000000000 | tf_op jit(solution)/shard_map/pallas_call | solution.py:259
  17.3 9.5 %all_to_all.15 = bf16[32,5,2,128]{3,2,1,0:T(2,128)(2,1)S(1)} all-to-all(bf16[32,5,2,128]{3,2,1,0:T(2,128)(2,1)S(1)} %bitcast.12), channel_id=1, replica_groups=mesh['rep'=2,'shard'=16] {'rep','shard'}, dimensions={0} | all-to-all | bytes 163840 | tf_op jit(solution)/shard_map/all_to_all | solution.py:238
  26.7 0.0 copy-done
  26.7 0.0 copy-done.1
  26.8 4.7 %shard_map.95 = (f32[8,128]{1,0:T(8,128)}, bf16[320,128]{1,0:T(8,128)(2,1)S(1)}, bf16[2,320,512]{2,1,0:T(8,128)(2,1)S(1)}) custom-call(s32[1,256]{1,0:T(1,128)S(1)} %get-tuple-element.16.order_ref, bf16[320,128]{1,0:T(8,128)(2,1)S(1)} %bitcast.9, bf16[256,320]{1,0:T(8,128)(2,1)S(1)} %get-tuple-element.18.take_ref, ...), custom_call_target="tpu_custom_call" | custom-call | tf_op jit(solution)/shard_map/pallas_call | solution.py:265
  31.4 9.2 %all_to_all.16 = bf16[32,5,2,128]{3,2,1,0:T(2,128)(2,1)S(1)} all-to-all(bf16[32,5,2,128]{3,2,1,0:T(2,128)(2,1)S(1)} %bitcast.11), channel_id=1, replica_groups=mesh['rep'=2,'shard'=16] {'rep','shard'}, dimensions={0} | all-to-all | bytes 163840 | tf_op jit(solution)/shard_map/all_to_all | solution.py:238
  40.6 1.1 %shard_map.96 = (f32[64,512]{1,0:T(8,128)}, f32[64,512]{1,0:T(8,128)}, f32[64,512]{1,0:T(8,128)}) custom-call(bf16[320,128]{1,0:T(8,128)(2,1)S(1)} %bitcast.10, bf16[2,320,512]{2,1,0:T(8,128)(2,1)S(1)} %get-tuple-element.22.hot_ref, f32[64,512]{1,0:T(8,128)S(1)} %get-tuple-element.23.zt_ref, f32[64,512]{1,0:T(8,128)S(1)} %get-tuple-element.24.nt_ref), custom_call_target="tpu_custom_call" | custom-call | tf_op jit(solution)/shard_map/pallas_call | solution.py:276
Async XLA Ops:
  1.9 14.5 %all-to-all-start = ((s32[32,2,128]{2,1,0:T(2,128)}), s32[32,2,128]{2,1,0:T(2,128)S(1)}, u32[]{:S(2)}, u32[]{:S(2)}) async-start(s32[32,2,128]{2,1,0:T(2,128)} %broadcast_in_dim.2), calls=%async_computation | async-start | bytes 65536 | tf_op jit(solution)/shard_map/all_to_all | solution.py:238
  16.4 10.3 %copy-start = (bf16[256,128,128]{2,1,0:T(8,128)(2,1)S(1)}, bf16[256,128,128]{2,1,0:T(8,128)(2,1)}, u32[]{:S(2)}) copy-start(bf16[256,128,128]{2,1,0:T(8,128)(2,1)} %tile_ref.1) | copy-start | bytes 25165828
  16.4 10.3 %copy-start.1 = (s32[8,128]{1,0:T(8,128)S(1)}, s32[8,128]{1,0:T(8,128)}, u32[]{:S(2)}) copy-start(s32[8,128]{1,0:T(8,128)} %labels_ref.1) | copy-start | bytes 12292

commit v5 on v4

--- a/solution.py
+++ b/solution.py
@@ -73,8 +73,11 @@
 
 
 def one_hot(column, blk):
-    shape = (column.shape[0], blk)
-    return mask(jnp.broadcast_to(column, shape) == iota(shape, 1))
+    shape = (column.shape[0], 128)
+    wide = jnp.broadcast_to(column, shape).astype(jnp.int16)
+    one, zero = jnp.ones(shape, bf16), jnp.zeros(shape, bf16)
+    parts = [jnp.where(wide == (iota(shape, 1) + at).astype(jnp.int16), one, zero) for at in range(0, blk, 128)]
+    return jnp.concatenate(parts, axis=1)
 
 
 def prepare_kernel(
@@ -138,46 +141,49 @@
     nt_ref[...] = jnp.where(rep == 0, nt[:half], nt[half:])
 
 
-def answer_kernel(lines, asked_ref, pull_ref, answer_ref):
+def answer_kernel(lines, asked_ref, pull_ref, answer_ref, hot_ref):
     blk, lane = pull_ref.shape
     me = lax.axis_index("shard")
     rep = lax.axis_index("rep")
     rank, local = asked_slots(asked_ref[...], me * blk, blk)
     (column,) = slot_rows(rank, local, lines, (rep * lines).astype(f32))
-    answer_ref[...] = jnp.dot(one_hot(column, blk), pull_ref[...], preferred_element_type=f32).astype(bf16)
+    hot = one_hot(column, blk)
+    hot_ref[...] = hot
+    answer_ref[...] = jnp.dot(hot, pull_ref[...], preferred_element_type=f32).astype(bf16)
 
 
 def worker_kernel(
-    lines, order_ref, answer_ref, take_ref, put_ref, labels_ref, asked_ref, tile_ref, margin_ref, out_ref, hot_ref,
-    w_ref, sum_ref, grad_ref
+    lines, order_vmem, answer_ref, take_ref, put_ref, labels_ref, asked_ref, tile_ref, margin_ref, out_ref, hot_ref,
+    w_ref, grad_ref, order_ref, sem
 ):
     tiles, lane, _ = tile_ref.shape
     groups = labels_ref.shape[0]
     each = tiles // groups
+    order_copy = pltpu.make_async_copy(order_vmem, order_ref, sem)
+    order_copy.start()
+    blk = hot_ref.shape[1]
+    rank, local = asked_slots(asked_ref[...], lax.axis_index("shard") * blk, blk)
+    other = (1 - lax.axis_index("rep")) * lines
+    (column,) = slot_rows(rank, local, lines, other.astype(f32))
+    hot_ref[...] = one_hot(column, blk)
     w_ref[...] = jnp.dot(take_ref[...], answer_ref[...], preferred_element_type=f32)
-    for g in range(groups):
-        def add(j, acc):
-            p = g * each + j
-            return acc + tile_ref[order_ref[0, p]].astype(f32) * w_ref[pl.ds(p, 1), :]
-
-        sum_ref[g] = lax.fori_loop(0, each, add, jnp.zeros((lane, lane), f32), unroll=8)
-    margins = jnp.concatenate([jnp.sum(sum_ref[g], axis=1).reshape(1, lane) for g in range(groups)], axis=0)
-    margin_ref[...] = margins
-    resid = (jax.nn.sigmoid(margins) - labels_ref[...].astype(f32)).astype(bf16)
-    rows, blk = hot_ref.shape[1:]
-    share = rows // groups
-    rank, local = asked_slots(asked_ref[...], lax.axis_index("shard") * blk, blk)
-    columns = slot_rows(rank, local, lines, 0.0, float(lines))
-    for g in range(groups):
-        for side, column in enumerate(columns):
-            hot_ref[side, g * share : (g + 1) * share] = one_hot(column[g * share : (g + 1) * share], blk)
-        row = resid[g : g + 1]
-        for j in range(0, each, 2):
-            p = g * each + j
-            pair = jnp.concatenate([tile_ref[order_ref[0, p]], tile_ref[order_ref[0, p + 1]]], axis=1)
-            both = jnp.dot(row, pair, preferred_element_type=f32)
-            grad_ref[p : p + 1, :] = both[:, :lane]
-            grad_ref[p + 1 : p + 2, :] = both[:, lane:]
+    order_copy.wait()
+    resid = None
+    for g in range(groups + 1):
+        if g < groups:
+            total = jnp.zeros((lane, lane), f32)
+            for p in range(g * each, (g + 1) * each):
+                total = total + tile_ref[order_ref[0, p]].astype(f32) * w_ref[p : p + 1, :]
+            margin = jnp.sum(total, axis=1).reshape(1, lane)
+            margin_ref[g : g + 1, :] = margin
+        if g > 0:
+            for p in range((g - 1) * each, g * each, 2):
+                pair = jnp.concatenate([tile_ref[order_ref[0, p]], tile_ref[order_ref[0, p + 1]]], axis=1)
+                both = jnp.dot(resid, pair, preferred_element_type=f32)
+                grad_ref[p : p + 1, :] = both[:, :lane]
+                grad_ref[p + 1 : p + 2, :] = both[:, lane:]
+        if g < groups:
+            resid = (jax.nn.sigmoid(margin) - labels_ref[g : g + 1, :].astype(f32)).astype(bf16)
     grads = grad_ref[...]
     half = lane // 2
     swapped = jnp.concatenate([grads[:, half:], grads[:, :half]], axis=1)
@@ -190,13 +196,14 @@
         out_ref[rep * sent.shape[0] : (rep + 1) * sent.shape[0]] = sent
 
 
-def update_kernel(incoming_ref, hot_ref, zt_ref, nt_ref, z_out, n_out, w_out):
+def update_kernel(incoming_ref, mine_ref, other_ref, zt_ref, nt_ref, z_out, n_out, w_out):
     half = zt_ref.shape[0]
     incoming = incoming_ref[...]
     over_rows = (((0,), (0,)), ((), ()))
-    left = lax.dot_general(incoming, hot_ref[0], over_rows, preferred_element_type=f32)
-    right = lax.dot_general(incoming, hot_ref[1], over_rows, preferred_element_type=f32)
-    total = left[:half] + right[half:]
+    mine = lax.dot_general(incoming, mine_ref[...], over_rows, preferred_element_type=f32)
+    other = lax.dot_general(incoming, other_ref[...], over_rows, preferred_element_type=f32)
+    first = lax.axis_index("rep") == 0
+    total = jnp.where(first, mine[:half] + other[half:], mine[half:] + other[:half])
     z_state = zt_ref[...]
     n_state = nt_ref[...]
     w_old = shrink(z_state, n_state)
@@ -256,24 +263,29 @@
         [pltpu.VMEM((parts, 128), i32)] * 2 + [pltpu.VMEM((blk, lane), f32)] * 2 + [pltpu.SemaphoreType.DMA((4,))],
         flops=4 * 10**9,
     )(*(in_hbm(x) for x in (ids, tile_group.reshape(parts, 128), z_state, n_state)))
-    answer = call(
+    answer, mine = call(
         functools.partial(answer_kernel, lines),
-        shape((devices * lines, lane), bf16),
+        (shape((devices * lines, lane), bf16), shape((devices * lines, blk), bf16)),
         [VMEM] * 2,
         flops=8 * 10**9,
     )(asked, pull)
-    margins, outgoing, hot = call(
+    margins, outgoing, other = call(
         functools.partial(worker_kernel, lines),
         (
             shape((groups, lane), f32),
             shape((devices * lines, lane), bf16),
-            shape((2, devices * lines, blk), bf16),
+            shape((devices * lines, blk), bf16),
         ),
-        [SMEM] + [VMEM] * 6,
-        [pltpu.VMEM((tiles, lane), f32), pltpu.VMEM((groups, lane, lane), f32), pltpu.VMEM((tiles, lane), f32)],
+        [VMEM] * 7,
+        [
+            pltpu.VMEM((tiles, lane), f32),
+            pltpu.VMEM((tiles, lane), f32),
+            pltpu.SMEM((1, tiles), i32),
+            pltpu.SemaphoreType.DMA,
+        ],
     )(order, swap_rows(answer), take, put, labels, asked, tile_values)
     incoming = swap_rows(outgoing)
-    outs = call(update_kernel, (shape((half, blk), f32),) * 3, [VMEM] * 4)(incoming, hot, zt, nt)
+    outs = call(update_kernel, (shape((half, blk), f32),) * 3, [VMEM] * 5)(incoming, mine, other, zt, nt)
     return (margins,) + tuple(o.T for o in outs)
 
 

time: 42 us -> 41.3 us (0.983)
  Pallas kernels: 8.12 us -> 7.39 us
    pallas_call x1, Pallas kernels: 4.69 us -> 3.96 us  [body(): call(functools.partial(worker_kernel, lines), (shape((groups, lane), f32)...]
  transfers between devices with their start and end apart: 1 -> 1, of which waited for: 1 -> 1; matrix products, arithmetic and copies ran while one was open for 0% -> 0% of each run, Pallas kernels for 3% -> 4%
where the time goes in v5:
time: 41.3 us; the launch traced here: 41.1 us
  blocking collectives  18.6 us (45%)
  Pallas kernels  7.39 us (18%)
  starting transfers between devices  7.3 us (18%)
  waiting for transfers between devices  5.75 us (14%)
  local copies, waits for them, and re-layouts  1.31 us (3%)
  between operations  0.66 us (2%)
    all_to_all x2, blocking collectives, swap(): lax.all_to_all(x, ('rep', 'shard'), split_axis=0, concat_axis=0, tiled=True)  18.6 us
    all_to_all x1, starting transfers between devices, swap(): lax.all_to_all(x, ('rep', 'shard'), split_axis=0, concat_axis=0, tiled=True)  7.3 us
    all_to_all x1, waiting for transfers between devices, swap(): lax.all_to_all(x, ('rep', 'shard'), split_axis=0, concat_axis=0, tiled=True)  5.75 us
    pallas_call x1, Pallas kernels, body(): call(functools.partial(worker_kernel, lines), (shape((groups, lane), f32)...  3.96 us
    pallas_call x1, Pallas kernels, body(): call(functools.partial(prepare_kernel, shards, groups, lines), (shape((bl...  1.44 us
    broadcast_in_dim x1, local copies, waits for them, and re-layouts, body(): asked = swap(jnp.broadcast_to(ids[None], (devices, parts, 128)))  1.3 us
    pallas_call x1, Pallas kernels, body(): call(update_kernel, (shape((half, blk), f32),) * 3, [VMEM] * 5)  1.16 us
    pallas_call x1, Pallas kernels, body(): call(functools.partial(answer_kernel, lines), (shape((devices * lines, la...  0.83 us
  transfers between devices with their start and end apart: 1, of which 1 were waited for; matrix products, arithmetic and copies ran while one was open for 0% of the time, Pallas kernels for 4%

profile of v5, /device:TPU:0, one launch (start us, length us, event | category | flops | bytes accessed | tf_op | source)
XLA Modules:
  0.0 41.1 jit_solution(13819016170310542456)
XLA Ops:
  0.6 1.3 %broadcast_in_dim.2 = s32[32,2,128]{2,1,0:T(2,128)} broadcast(s32[2,128]{1,0:T(2,128)} %bitcast.13), dimensions={1,2} | broadcast | bytes 33792 | tf_op jit(solution)/shard_map/broadcast_in_dim | solution.py:251
  1.9 7.3 %all-to-all-start = ((s32[32,2,128]{2,1,0:T(2,128)}), s32[32,2,128]{2,1,0:T(2,128)S(1)}, u32[]{:S(2)}, u32[]{:S(2)}) async-start(s32[32,2,128]{2,1,0:T(2,128)} %broadcast_in_dim.2), calls=%async_computation | async-start | bytes 65536 | tf_op jit(solution)/shard_map/all_to_all | solution.py:245
  9.2 1.4 %shard_map.93 = (bf16[512,128]{1,0:T(8,128)(2,1)S(1)}, s32[1,256]{1,0:T(1,128)S(1)}, bf16[256,320]{1,0:T(8,128)(2,1)S(1)}, bf16[160,512]{1,0:T(8,128)(2,1)S(1)},...) custom-call(s32[2,128]{1,0:T(2,128)} %bitcast.14, s32[2,128]{1,0:T(2,128)} %bitcast.18, f32[512,128]{1,0:T(8,128)} %z_hbm.1, ...), custom_call_target="tpu_custom_call" | custom-call | flops 4000000000 | tf_op jit(solution)/shard_map/pallas_call | solution.py:252
  10.7 5.8 %all-to-all-done.asked_ref = s32[32,2,128]{2,1,0:T(2,128)S(1)} async-done(((s32[32,2,128]{2,1,0:T(2,128)}), s32[32,2,128]{2,1,0:T(2,128)S(1)}, u32[]{:S(2)}, u32[]{:S(2)}) %all-to-all-start) | async-done | bytes 32800 | tf_op jit(solution)/shard_map/all_to_all | solution.py:245
  16.4 0.0 copy-start
  16.4 0.0 copy-start.1
  16.4 0.8 %shard_map.94 = (bf16[320,128]{1,0:T(8,128)(2,1)S(1)}, bf16[320,512]{1,0:T(8,128)(2,1)S(1)}) custom-call(s32[32,2,128]{2,1,0:T(2,128)S(1)} %all-to-all-done.asked_ref, bf16[512,128]{1,0:T(8,128)(2,1)S(1)} %get-tuple-element.19.pull_ref), custom_call_target="tpu_custom_call" | custom-call | flops 8000000000 | tf_op jit(solution)/shard_map/pallas_call | solution.py:266
  17.3 9.5 %all_to_all.15 = bf16[32,5,2,128]{3,2,1,0:T(2,128)(2,1)S(1)} all-to-all(bf16[32,5,2,128]{3,2,1,0:T(2,128)(2,1)S(1)} %bitcast.12), channel_id=1, replica_groups=mesh['rep'=2,'shard'=16] {'rep','shard'}, dimensions={0} | all-to-all | bytes 163840 | tf_op jit(solution)/shard_map/all_to_all | solution.py:245
  26.7 0.0 copy-done
  26.7 0.0 copy-done.1
  26.7 4.0 %shard_map.95 = (f32[8,128]{1,0:T(8,128)}, bf16[320,128]{1,0:T(8,128)(2,1)S(1)}, bf16[320,512]{1,0:T(8,128)(2,1)S(1)}) custom-call(s32[1,256]{1,0:T(1,128)S(1)} %get-tuple-element.18.order_vmem, bf16[320,128]{1,0:T(8,128)(2,1)S(1)} %bitcast.9, bf16[256,320]{1,0:T(8,128)(2,1)S(1)} %get-tuple-element.21.take_ref, ...), custom_call_target="tpu_custom_call" | custom-call | tf_op jit(solution)/shard_map/pallas_call | solution.py:272
  30.7 9.2 %all_to_all.16 = bf16[32,5,2,128]{3,2,1,0:T(2,128)(2,1)S(1)} all-to-all(bf16[32,5,2,128]{3,2,1,0:T(2,128)(2,1)S(1)} %bitcast.11), channel_id=1, replica_groups=mesh['rep'=2,'shard'=16] {'rep','shard'}, dimensions={0} | all-to-all | bytes 163840 | tf_op jit(solution)/shard_map/all_to_all | solution.py:245
  39.9 1.2 %shard_map.96 = (f32[64,512]{1,0:T(8,128)}, f32[64,512]{1,0:T(8,128)}, f32[64,512]{1,0:T(8,128)}) custom-call(bf16[320,128]{1,0:T(8,128)(2,1)S(1)} %bitcast.10, bf16[320,512]{1,0:T(8,128)(2,1)S(1)} %get-tuple-element.25.mine_ref, bf16[320,512]{1,0:T(8,128)(2,1)S(1)} %get-tuple-element.26.other_ref, f32[64,512]{1,0:T(8,128)S(1)} %get-tuple-element.27.zt_ref, ...), custom_call_target="tpu_custom_call" | custom-call | tf_op jit(solution)/shard_map/pallas_call | solution.py:288
Async XLA Ops:
  1.9 14.5 %all-to-all-start = ((s32[32,2,128]{2,1,0:T(2,128)}), s32[32,2,128]{2,1,0:T(2,128)S(1)}, u32[]{:S(2)}, u32[]{:S(2)}) async-start(s32[32,2,128]{2,1,0:T(2,128)} %broadcast_in_dim.2), calls=%async_computation | async-start | bytes 65536 | tf_op jit(solution)/shard_map/all_to_all | solution.py:245
  16.4 10.3 %copy-start = (bf16[256,128,128]{2,1,0:T(8,128)(2,1)S(1)}, bf16[256,128,128]{2,1,0:T(8,128)(2,1)}, u32[]{:S(2)}) copy-start(bf16[256,128,128]{2,1,0:T(8,128)(2,1)} %tile_ref.1) | copy-start | bytes 25165828
  16.4 10.3 %copy-start.1 = (s32[8,128]{1,0:T(8,128)S(1)}, s32[8,128]{1,0:T(8,128)}, u32[]{:S(2)}) copy-start(s32[8,128]{1,0:T(8,128)} %labels_ref.1) | copy-start | bytes 12292

commit v6 on v5

--- a/solution.py
+++ b/solution.py
@@ -36,19 +36,10 @@
 
 
 def asked_slots(asked, first, blk):
-    tri = before(128)
-    count = 0.0
-    ranks = []
-    locals_ = []
-    for part in range(asked.shape[1]):
-        local = asked[:, part, :] - first
-        valid = (local >= 0) & (local < blk)
-        ones = valid.astype(f32)
-        rank = jnp.dot(ones.astype(bf16), tri, preferred_element_type=f32) + count
-        count = count + jnp.sum(ones, axis=1, keepdims=True)
-        ranks.append(jnp.where(valid, rank, -1.0))
-        locals_.append(jnp.where(valid, local, 0))
-    return jnp.concatenate(ranks, axis=1), jnp.concatenate(locals_, axis=1)
+    local = jnp.concatenate([asked[:, part, :] for part in range(asked.shape[1])], axis=1) - first
+    valid = (local >= 0) & (local < blk)
+    rank = jnp.dot(mask(valid), before(local.shape[1]), preferred_element_type=f32)
+    return jnp.where(valid, rank, -1.0), jnp.where(valid, local, 0)
 
 
 def slot_rows(rank, local, lines, *firsts):
@@ -61,10 +52,10 @@
     number = local + 1
     high = number // 256
     low = number - high * 256
-    each_rank = jnp.dot(spread, rank.astype(bf16), preferred_element_type=f32)
-    each_high = jnp.dot(spread, high.astype(f32).astype(bf16), preferred_element_type=f32)
-    each_low = jnp.dot(spread, low.astype(f32).astype(bf16), preferred_element_type=f32)
-    each = each_high * 256.0 + each_low
+    facts = jnp.concatenate([rank, high.astype(f32), low.astype(f32)], axis=1).astype(bf16)
+    facts = jnp.dot(spread, facts, preferred_element_type=f32)
+    each_rank = facts[:, :tiles]
+    each = facts[:, tiles : 2 * tiles] * 256.0 + facts[:, 2 * tiles :]
     columns = []
     for first in firsts:
         picked = jnp.where(each_rank - first == line, each, 0.0)
@@ -82,7 +73,7 @@
 
 def prepare_kernel(
     shards, groups, lines, block_hbm, group_hbm, z_hbm, n_hbm, pull_ref, order_ref, take_ref, put_ref, zt_ref, nt_ref,
-    block_ref, group_ref, z_ref, n_ref, sem
+    wt_ref, rt_ref,    block_ref, group_ref, z_ref, n_ref, sem
 ):
     copies = [
         pltpu.make_async_copy(source, target, sem.at[i])
@@ -137,8 +128,12 @@
     pull_ref[...] = shrink(z_ref[...], n_ref[...]).astype(bf16)
     zt = z_ref[...].T
     nt = n_ref[...].T
-    zt_ref[...] = jnp.where(rep == 0, zt[:half], zt[half:])
-    nt_ref[...] = jnp.where(rep == 0, nt[:half], nt[half:])
+    zt = jnp.where(rep == 0, zt[:half], zt[half:])
+    nt = jnp.where(rep == 0, nt[:half], nt[half:])
+    zt_ref[...] = zt
+    nt_ref[...] = nt
+    wt_ref[...] = shrink(zt, nt)
+    rt_ref[...] = jnp.sqrt(nt)
 
 
 def answer_kernel(lines, asked_ref, pull_ref, answer_ref, hot_ref):
@@ -153,13 +148,14 @@
 
 
 def worker_kernel(
-    lines, order_vmem, answer_ref, take_ref, put_ref, labels_ref, asked_ref, tile_ref, margin_ref, out_ref, hot_ref,
-    w_ref, grad_ref, order_ref, sem
+    lines, order_vmem, answer_ref, take_ref, put_ref, labels_ref, asked_ref, tile_ref, margin_hbm, out_ref, hot_ref,
+    w_ref, grad_ref, margin_ref, order_ref, sem
 ):
     tiles, lane, _ = tile_ref.shape
     groups = labels_ref.shape[0]
     each = tiles // groups
-    order_copy = pltpu.make_async_copy(order_vmem, order_ref, sem)
+    order_copy = pltpu.make_async_copy(order_vmem, order_ref, sem.at[0])
+    margin_copy = pltpu.make_async_copy(margin_ref, margin_hbm, sem.at[1])
     order_copy.start()
     blk = hot_ref.shape[1]
     rank, local = asked_slots(asked_ref[...], lax.axis_index("shard") * blk, blk)
@@ -176,6 +172,8 @@
                 total = total + tile_ref[order_ref[0, p]].astype(f32) * w_ref[p : p + 1, :]
             margin = jnp.sum(total, axis=1).reshape(1, lane)
             margin_ref[g : g + 1, :] = margin
+        if g == groups - 1:
+            margin_copy.start()
         if g > 0:
             for p in range((g - 1) * each, g * each, 2):
                 pair = jnp.concatenate([tile_ref[order_ref[0, p]], tile_ref[order_ref[0, p + 1]]], axis=1)
@@ -194,9 +192,10 @@
         sides = jnp.concatenate([jnp.where(left, first, 0.0), jnp.where(left, 0.0, second)], axis=0)
         sent = jnp.dot(put, sides.astype(bf16), preferred_element_type=f32).astype(bf16)
         out_ref[rep * sent.shape[0] : (rep + 1) * sent.shape[0]] = sent
-
-
-def update_kernel(incoming_ref, mine_ref, other_ref, zt_ref, nt_ref, z_out, n_out, w_out):
+    margin_copy.wait()
+
+
+def update_kernel(incoming_ref, mine_ref, other_ref, zt_ref, nt_ref, wt_ref, rt_ref, z_out, n_out, w_out):
     half = zt_ref.shape[0]
     incoming = incoming_ref[...]
     over_rows = (((0,), (0,)), ((), ()))
@@ -206,21 +205,20 @@
     total = jnp.where(first, mine[:half] + other[half:], mine[half:] + other[:half])
     z_state = zt_ref[...]
     n_state = nt_ref[...]
-    w_old = shrink(z_state, n_state)
     new_n = n_state + total * total
-    sigma = (jnp.sqrt(new_n) - jnp.sqrt(n_state)) / rate_alpha
-    new_z = z_state + total - sigma * w_old
+    sigma = (jnp.sqrt(new_n) - rt_ref[...]) / rate_alpha
+    new_z = z_state + total - sigma * wt_ref[...]
     z_out[...] = new_z
     n_out[...] = new_n
     w_out[...] = shrink(new_z, new_n)
 
 
-def call(kernel, out, specs, scratch=(), limit=16 << 20, flops=0):
+def call(kernel, out, specs, scratch=(), limit=16 << 20, flops=0, out_specs=None):
     return pl.pallas_call(
         kernel,
         out_shape=out,
         in_specs=specs,
-        out_specs=jax.tree.map(lambda _: VMEM, out),
+        out_specs=jax.tree.map(lambda _: VMEM, out) if out_specs is None else out_specs,
         scratch_shapes=list(scratch),
         compiler_params=pltpu.CompilerParams(vmem_limit_bytes=limit),
         cost_estimate=pl.CostEstimate(flops=flops, bytes_accessed=0, transcendentals=0),
@@ -249,16 +247,15 @@
 
     ids = tile_block.reshape(parts, 128)
     asked = swap(jnp.broadcast_to(ids[None], (devices, parts, 128)))
-    pull, order, take, put, zt, nt = call(
+    pull, order, take, put, *state = call(
         functools.partial(prepare_kernel, shards, groups, lines),
         (
             shape((blk, lane), bf16),
             shape((1, tiles), i32),
             shape((tiles, devices * lines), bf16),
             shape((shards * lines, 2 * tiles), bf16),
-            shape((half, blk), f32),
-            shape((half, blk), f32),
-        ),
+        )
+        + (shape((half, blk), f32),) * 4,
         [HBM] * 4,
         [pltpu.VMEM((parts, 128), i32)] * 2 + [pltpu.VMEM((blk, lane), f32)] * 2 + [pltpu.SemaphoreType.DMA((4,))],
         flops=4 * 10**9,
@@ -280,12 +277,14 @@
         [
             pltpu.VMEM((tiles, lane), f32),
             pltpu.VMEM((tiles, lane), f32),
+            pltpu.VMEM((groups, lane), f32),
             pltpu.SMEM((1, tiles), i32),
-            pltpu.SemaphoreType.DMA,
+            pltpu.SemaphoreType.DMA((2,)),
         ],
+        out_specs=(HBM, VMEM, VMEM),
     )(order, swap_rows(answer), take, put, labels, asked, tile_values)
     incoming = swap_rows(outgoing)
-    outs = call(update_kernel, (shape((half, blk), f32),) * 3, [VMEM] * 5)(incoming, mine, other, zt, nt)
+    outs = call(update_kernel, (shape((half, blk), f32),) * 3, [VMEM] * 7)(incoming, mine, other, *state)
     return (margins,) + tuple(o.T for o in outs)
 
 

time: 41.3 us -> 41.2 us (level)
  no operation moved by 1% of the time
where the time goes in v6:
time: 41.2 us; the launch traced here: 40.9 us
  blocking collectives  18.6 us (45%)
  starting transfers between devices  7.3 us (18%)
  Pallas kernels  7.29 us (18%)
  waiting for transfers between devices  5.73 us (14%)
  local copies, waits for them, and re-layouts  1.31 us (3%)
  between operations  0.66 us (2%)
    all_to_all x2, blocking collectives, swap(): lax.all_to_all(x, ('rep', 'shard'), split_axis=0, concat_axis=0, tiled=True)  18.6 us
    all_to_all x1, starting transfers between devices, swap(): lax.all_to_all(x, ('rep', 'shard'), split_axis=0, concat_axis=0, tiled=True)  7.3 us
    all_to_all x1, waiting for transfers between devices, swap(): lax.all_to_all(x, ('rep', 'shard'), split_axis=0, concat_axis=0, tiled=True)  5.73 us
    pallas_call x1, Pallas kernels, body(): call(functools.partial(worker_kernel, lines), (shape((groups, lane), f32)...  3.98 us
    pallas_call x1, Pallas kernels, body(): call(functools.partial(prepare_kernel, shards, groups, lines), (shape((bl...  1.47 us
    broadcast_in_dim x1, local copies, waits for them, and re-layouts, body(): asked = swap(jnp.broadcast_to(ids[None], (devices, parts, 128)))  1.3 us
    pallas_call x1, Pallas kernels, body(): call(update_kernel, (shape((half, blk), f32),) * 3, [VMEM] * 7)  1.14 us
  transfers between devices with their start and end apart: 1, of which 1 were waited for; matrix products, arithmetic and copies ran while one was open for 0% of the time, Pallas kernels for 4%

profile of v6, /device:TPU:0, one launch (start us, length us, event | category | flops | bytes accessed | tf_op | source)
XLA Modules:
  0.0 40.9 jit_solution(5736650833484247663)
XLA Ops:
  0.6 1.3 %broadcast_in_dim.2 = s32[32,2,128]{2,1,0:T(2,128)} broadcast(s32[2,128]{1,0:T(2,128)} %bitcast.13), dimensions={1,2} | broadcast | bytes 33792 | tf_op jit(solution)/shard_map/broadcast_in_dim | solution.py:249
  1.9 7.3 %all-to-all-start = ((s32[32,2,128]{2,1,0:T(2,128)}), s32[32,2,128]{2,1,0:T(2,128)S(1)}, u32[]{:S(2)}, u32[]{:S(2)}) async-start(s32[32,2,128]{2,1,0:T(2,128)} %broadcast_in_dim.2), calls=%async_computation | async-start | bytes 65536 | tf_op jit(solution)/shard_map/all_to_all | solution.py:243
  9.2 1.5 %shard_map.93 = (bf16[512,128]{1,0:T(8,128)(2,1)S(1)}, s32[1,256]{1,0:T(1,128)S(1)}, bf16[256,320]{1,0:T(8,128)(2,1)S(1)}, bf16[160,512]{1,0:T(8,128)(2,1)S(1)},...) custom-call(s32[2,128]{1,0:T(2,128)} %bitcast.14, ...), custom_call_target="tpu_custom_call" | custom-call | flops 4000000000 | tf_op jit(solution)/shard_map/pallas_call | solution.py:250
  10.7 5.7 %all-to-all-done.asked_ref = s32[32,2,128]{2,1,0:T(2,128)S(1)} async-done(((s32[32,2,128]{2,1,0:T(2,128)}), s32[32,2,128]{2,1,0:T(2,128)S(1)}, u32[]{:S(2)}, u32[]{:S(2)}) %all-to-all-start) | async-done | bytes 32800 | tf_op jit(solution)/shard_map/all_to_all | solution.py:243
  16.4 0.0 copy-start
  16.4 0.0 copy-start.1
  16.4 0.7 %shard_map.94 = (bf16[320,128]{1,0:T(8,128)(2,1)S(1)}, bf16[320,512]{1,0:T(8,128)(2,1)S(1)}) custom-call(s32[32,2,128]{2,1,0:T(2,128)S(1)} %all-to-all-done.asked_ref, bf16[512,128]{1,0:T(8,128)(2,1)S(1)} %get-tuple-element.21.pull_ref), custom_call_target="tpu_custom_call" | custom-call | flops 8000000000 | tf_op jit(solution)/shard_map/pallas_call | solution.py:263
  17.2 9.5 %all_to_all.15 = bf16[32,5,2,128]{3,2,1,0:T(2,128)(2,1)S(1)} all-to-all(bf16[32,5,2,128]{3,2,1,0:T(2,128)(2,1)S(1)} %bitcast.12), channel_id=1, replica_groups=mesh['rep'=2,'shard'=16] {'rep','shard'}, dimensions={0} | all-to-all | bytes 163840 | tf_op jit(solution)/shard_map/all_to_all | solution.py:243
  26.6 0.0 copy-done
  26.6 0.0 copy-done.1
  26.6 4.0 %shard_map.95 = (f32[8,128]{1,0:T(8,128)}, bf16[320,128]{1,0:T(8,128)(2,1)S(1)}, bf16[320,512]{1,0:T(8,128)(2,1)S(1)}) custom-call(s32[1,256]{1,0:T(1,128)S(1)} %get-tuple-element.20.order_vmem, bf16[320,128]{1,0:T(8,128)(2,1)S(1)} %bitcast.9, bf16[256,320]{1,0:T(8,128)(2,1)S(1)} %get-tuple-element.23.take_ref, ...), custom_call_target="tpu_custom_call" | custom-call | tf_op jit(solution)/shard_map/pallas_call | solution.py:269
  30.6 9.2 %all_to_all.16 = bf16[32,5,2,128]{3,2,1,0:T(2,128)(2,1)S(1)} all-to-all(bf16[32,5,2,128]{3,2,1,0:T(2,128)(2,1)S(1)} %bitcast.11), channel_id=1, replica_groups=mesh['rep'=2,'shard'=16] {'rep','shard'}, dimensions={0} | all-to-all | bytes 163840 | tf_op jit(solution)/shard_map/all_to_all | solution.py:243
  39.8 1.1 %shard_map.96 = (f32[64,512]{1,0:T(8,128)}, f32[64,512]{1,0:T(8,128)}, f32[64,512]{1,0:T(8,128)}) custom-call(bf16[320,128]{1,0:T(8,128)(2,1)S(1)} %bitcast.10, bf16[320,512]{1,0:T(8,128)(2,1)S(1)} %get-tuple-element.27.mine_ref, bf16[320,512]{1,0:T(8,128)(2,1)S(1)} %get-tuple-element.28.other_ref, f32[64,512]{1,0:T(8,128)S(1)} %get-tuple-element.29.zt_ref, ...), custom_call_target="tpu_custom_call" | custom-call | tf_op jit(solution)/shard_map/pallas_call | solution.py:287
Async XLA Ops:
  1.9 14.5 %all-to-all-start = ((s32[32,2,128]{2,1,0:T(2,128)}), s32[32,2,128]{2,1,0:T(2,128)S(1)}, u32[]{:S(2)}, u32[]{:S(2)}) async-start(s32[32,2,128]{2,1,0:T(2,128)} %broadcast_in_dim.2), calls=%async_computation | async-start | bytes 65536 | tf_op jit(solution)/shard_map/all_to_all | solution.py:243
  16.4 10.2 %copy-start = (bf16[256,128,128]{2,1,0:T(8,128)(2,1)S(1)}, bf16[256,128,128]{2,1,0:T(8,128)(2,1)}, u32[]{:S(2)}) copy-start(bf16[256,128,128]{2,1,0:T(8,128)(2,1)} %tile_ref.1) | copy-start | bytes 25165828
  16.4 10.2 %copy-start.1 = (s32[8,128]{1,0:T(8,128)S(1)}, s32[8,128]{1,0:T(8,128)}, u32[]{:S(2)}) copy-start(s32[8,128]{1,0:T(8,128)} %labels_ref.1) | copy-start | bytes 12292

commit v7 on v6

--- a/solution.py
+++ b/solution.py
@@ -164,7 +164,7 @@
     hot_ref[...] = one_hot(column, blk)
     w_ref[...] = jnp.dot(take_ref[...], answer_ref[...], preferred_element_type=f32)
     order_copy.wait()
-    resid = None
+    resid = []
     for g in range(groups + 1):
         if g < groups:
             total = jnp.zeros((lane, lane), f32)
@@ -172,16 +172,15 @@
                 total = total + tile_ref[order_ref[0, p]].astype(f32) * w_ref[p : p + 1, :]
             margin = jnp.sum(total, axis=1).reshape(1, lane)
             margin_ref[g : g + 1, :] = margin
+            resid.append((jax.nn.sigmoid(margin) - labels_ref[g : g + 1, :].astype(f32)).astype(bf16))
         if g == groups - 1:
             margin_copy.start()
         if g > 0:
             for p in range((g - 1) * each, g * each, 2):
                 pair = jnp.concatenate([tile_ref[order_ref[0, p]], tile_ref[order_ref[0, p + 1]]], axis=1)
-                both = jnp.dot(resid, pair, preferred_element_type=f32)
+                both = jnp.dot(resid[g - 1], pair, preferred_element_type=f32)
                 grad_ref[p : p + 1, :] = both[:, :lane]
                 grad_ref[p + 1 : p + 2, :] = both[:, lane:]
-        if g < groups:
-            resid = (jax.nn.sigmoid(margin) - labels_ref[g : g + 1, :].astype(f32)).astype(bf16)
     grads = grad_ref[...]
     half = lane // 2
     swapped = jnp.concatenate([grads[:, half:], grads[:, :half]], axis=1)
@@ -198,11 +197,11 @@
 def update_kernel(incoming_ref, mine_ref, other_ref, zt_ref, nt_ref, wt_ref, rt_ref, z_out, n_out, w_out):
     half = zt_ref.shape[0]
     incoming = incoming_ref[...]
-    over_rows = (((0,), (0,)), ((), ()))
-    mine = lax.dot_general(incoming, mine_ref[...], over_rows, preferred_element_type=f32)
-    other = lax.dot_general(incoming, other_ref[...], over_rows, preferred_element_type=f32)
+    turned = incoming.T
     first = lax.axis_index("rep") == 0
-    total = jnp.where(first, mine[:half] + other[half:], mine[half:] + other[:half])
+    mine = jnp.dot(jnp.where(first, turned[:half], turned[half:]), mine_ref[...], preferred_element_type=f32)
+    other = jnp.dot(jnp.where(first, turned[half:], turned[:half]), other_ref[...], preferred_element_type=f32)
+    total = mine + other
     z_state = zt_ref[...]
     n_state = nt_ref[...]
     new_n = n_state + total * total

time: 41.2 us -> 41.1 us (level)
  no operation moved by 1% of the time
where the time goes in v7:
time: 41.1 us; the launch traced here: 40.9 us
  blocking collectives  18.6 us (45%)
  starting transfers between devices  7.3 us (18%)
  Pallas kernels  7.24 us (18%)
  waiting for transfers between devices  5.73 us (14%)
  local copies, waits for them, and re-layouts  1.31 us (3%)
  between operations  0.66 us (2%)
    all_to_all x2, blocking collectives, swap(): lax.all_to_all(x, ('rep', 'shard'), split_axis=0, concat_axis=0, tiled=True)  18.6 us
    all_to_all x1, starting transfers between devices, swap(): lax.all_to_all(x, ('rep', 'shard'), split_axis=0, concat_axis=0, tiled=True)  7.3 us
    all_to_all x1, waiting for transfers between devices, swap(): lax.all_to_all(x, ('rep', 'shard'), split_axis=0, concat_axis=0, tiled=True)  5.73 us
    pallas_call x1, Pallas kernels, body(): call(functools.partial(worker_kernel, lines), (shape((groups, lane), f32)...  3.98 us
    pallas_call x1, Pallas kernels, body(): call(functools.partial(prepare_kernel, shards, groups, lines), (shape((bl...  1.47 us
    broadcast_in_dim x1, local copies, waits for them, and re-layouts, body(): asked = swap(jnp.broadcast_to(ids[None], (devices, parts, 128)))  1.3 us
    pallas_call x1, Pallas kernels, body(): call(update_kernel, (shape((half, blk), f32),) * 3, [VMEM] * 7)  1.09 us
  transfers between devices with their start and end apart: 1, of which 1 were waited for; matrix products, arithmetic and copies ran while one was open for 0% of the time, Pallas kernels for 4%

profile of v7, /device:TPU:0, one launch (start us, length us, event | category | flops | bytes accessed | tf_op | source)
XLA Modules:
  0.0 40.9 jit_solution(4216272403228867497)
XLA Ops:
  0.6 1.3 %broadcast_in_dim.2 = s32[32,2,128]{2,1,0:T(2,128)} broadcast(s32[2,128]{1,0:T(2,128)} %bitcast.13), dimensions={1,2} | broadcast | bytes 33792 | tf_op jit(solution)/shard_map/broadcast_in_dim | solution.py:248
  1.9 7.3 %all-to-all-start = ((s32[32,2,128]{2,1,0:T(2,128)}), s32[32,2,128]{2,1,0:T(2,128)S(1)}, u32[]{:S(2)}, u32[]{:S(2)}) async-start(s32[32,2,128]{2,1,0:T(2,128)} %broadcast_in_dim.2), calls=%async_computation | async-start | bytes 65536 | tf_op jit(solution)/shard_map/all_to_all | solution.py:242
  9.2 1.5 %shard_map.93 = (bf16[512,128]{1,0:T(8,128)(2,1)S(1)}, s32[1,256]{1,0:T(1,128)S(1)}, bf16[256,320]{1,0:T(8,128)(2,1)S(1)}, bf16[160,512]{1,0:T(8,128)(2,1)S(1)},...) custom-call(s32[2,128]{1,0:T(2,128)} %bitcast.14, ...), custom_call_target="tpu_custom_call" | custom-call | flops 4000000000 | tf_op jit(solution)/shard_map/pallas_call | solution.py:249
  10.7 5.7 %all-to-all-done.asked_ref = s32[32,2,128]{2,1,0:T(2,128)S(1)} async-done(((s32[32,2,128]{2,1,0:T(2,128)}), s32[32,2,128]{2,1,0:T(2,128)S(1)}, u32[]{:S(2)}, u32[]{:S(2)}) %all-to-all-start) | async-done | bytes 32800 | tf_op jit(solution)/shard_map/all_to_all | solution.py:242
  16.4 0.0 copy-start
  16.4 0.0 copy-start.1
  16.4 0.7 %shard_map.94 = (bf16[320,128]{1,0:T(8,128)(2,1)S(1)}, bf16[320,512]{1,0:T(8,128)(2,1)S(1)}) custom-call(s32[32,2,128]{2,1,0:T(2,128)S(1)} %all-to-all-done.asked_ref, bf16[512,128]{1,0:T(8,128)(2,1)S(1)} %get-tuple-element.21.pull_ref), custom_call_target="tpu_custom_call" | custom-call | flops 8000000000 | tf_op jit(solution)/shard_map/pallas_call | solution.py:262
  17.2 9.5 %all_to_all.15 = bf16[32,5,2,128]{3,2,1,0:T(2,128)(2,1)S(1)} all-to-all(bf16[32,5,2,128]{3,2,1,0:T(2,128)(2,1)S(1)} %bitcast.12), channel_id=1, replica_groups=mesh['rep'=2,'shard'=16] {'rep','shard'}, dimensions={0} | all-to-all | bytes 163840 | tf_op jit(solution)/shard_map/all_to_all | solution.py:242
  26.6 0.0 copy-done
  26.6 0.0 copy-done.1
  26.6 4.0 %shard_map.95 = (f32[8,128]{1,0:T(8,128)}, bf16[320,128]{1,0:T(8,128)(2,1)S(1)}, bf16[320,512]{1,0:T(8,128)(2,1)S(1)}) custom-call(s32[1,256]{1,0:T(1,128)S(1)} %get-tuple-element.20.order_vmem, bf16[320,128]{1,0:T(8,128)(2,1)S(1)} %bitcast.9, bf16[256,320]{1,0:T(8,128)(2,1)S(1)} %get-tuple-element.23.take_ref, ...), custom_call_target="tpu_custom_call" | custom-call | tf_op jit(solution)/shard_map/pallas_call | solution.py:268
  30.6 9.2 %all_to_all.16 = bf16[32,5,2,128]{3,2,1,0:T(2,128)(2,1)S(1)} all-to-all(bf16[32,5,2,128]{3,2,1,0:T(2,128)(2,1)S(1)} %bitcast.11), channel_id=1, replica_groups=mesh['rep'=2,'shard'=16] {'rep','shard'}, dimensions={0} | all-to-all | bytes 163840 | tf_op jit(solution)/shard_map/all_to_all | solution.py:242
  39.8 1.1 %shard_map.96 = (f32[64,512]{1,0:T(8,128)}, f32[64,512]{1,0:T(8,128)}, f32[64,512]{1,0:T(8,128)}) custom-call(bf16[320,128]{1,0:T(8,128)(2,1)S(1)} %bitcast.10, bf16[320,512]{1,0:T(8,128)(2,1)S(1)} %get-tuple-element.27.mine_ref, bf16[320,512]{1,0:T(8,128)(2,1)S(1)} %get-tuple-element.28.other_ref, f32[64,512]{1,0:T(8,128)S(1)} %get-tuple-element.29.zt_ref, ...), custom_call_target="tpu_custom_call" | custom-call | tf_op jit(solution)/shard_map/pallas_call | solution.py:286
Async XLA Ops:
  1.9 14.5 %all-to-all-start = ((s32[32,2,128]{2,1,0:T(2,128)}), s32[32,2,128]{2,1,0:T(2,128)S(1)}, u32[]{:S(2)}, u32[]{:S(2)}) async-start(s32[32,2,128]{2,1,0:T(2,128)} %broadcast_in_dim.2), calls=%async_computation | async-start | bytes 65536 | tf_op jit(solution)/shard_map/all_to_all | solution.py:242
  16.4 10.2 %copy-start = (bf16[256,128,128]{2,1,0:T(8,128)(2,1)S(1)}, bf16[256,128,128]{2,1,0:T(8,128)(2,1)}, u32[]{:S(2)}) copy-start(bf16[256,128,128]{2,1,0:T(8,128)(2,1)} %tile_ref.1) | copy-start | bytes 25165828
  16.4 10.2 %copy-start.1 = (s32[8,128]{1,0:T(8,128)S(1)}, s32[8,128]{1,0:T(8,128)}, u32[]{:S(2)}) copy-start(s32[8,128]{1,0:T(8,128)} %labels_ref.1) | copy-start | bytes 12292

commit v8 on v7

--- a/solution.py
+++ b/solution.py
@@ -168,9 +168,15 @@
     for g in range(groups + 1):
         if g < groups:
             total = jnp.zeros((lane, lane), f32)
-            for p in range(g * each, (g + 1) * each):
+            whole = (g + 1) * each - 2
+            for p in range(g * each, whole):
                 total = total + tile_ref[order_ref[0, p]].astype(f32) * w_ref[p : p + 1, :]
             margin = jnp.sum(total, axis=1).reshape(1, lane)
+            for p in range(whole, (g + 1) * each):
+                weights = w_ref[p : p + 1, :].astype(bf16)
+                margin = margin + lax.dot_general(
+                    weights, tile_ref[order_ref[0, p]], (((1,), (1,)), ((), ())), preferred_element_type=f32
+                )
             margin_ref[g : g + 1, :] = margin
             resid.append((jax.nn.sigmoid(margin) - labels_ref[g : g + 1, :].astype(f32)).astype(bf16))
         if g == groups - 1:

time: 41.1 us -> 41.1 us (level)
  no operation moved by 1% of the time
where the time goes in v8:
time: 41.1 us; the launch traced here: 40.8 us
  blocking collectives  18.6 us (45%)
  starting transfers between devices  7.3 us (18%)
  Pallas kernels  7.19 us (17%)
  waiting for transfers between devices  5.73 us (14%)
  local copies, waits for them, and re-layouts  1.31 us (3%)
  between operations  0.66 us (2%)
    all_to_all x2, blocking collectives, swap(): lax.all_to_all(x, ('rep', 'shard'), split_axis=0, concat_axis=0, tiled=True)  18.6 us
    all_to_all x1, starting transfers between devices, swap(): lax.all_to_all(x, ('rep', 'shard'), split_axis=0, concat_axis=0, tiled=True)  7.3 us
    all_to_all x1, waiting for transfers between devices, swap(): lax.all_to_all(x, ('rep', 'shard'), split_axis=0, concat_axis=0, tiled=True)  5.73 us
    pallas_call x1, Pallas kernels, body(): call(functools.partial(worker_kernel, lines), (shape((groups, lane), f32)...  3.94 us
    pallas_call x1, Pallas kernels, body(): call(functools.partial(prepare_kernel, shards, groups, lines), (shape((bl...  1.47 us
    broadcast_in_dim x1, local copies, waits for them, and re-layouts, body(): asked = swap(jnp.broadcast_to(ids[None], (devices, parts, 128)))  1.3 us
    pallas_call x1, Pallas kernels, body(): call(update_kernel, (shape((half, blk), f32),) * 3, [VMEM] * 7)  1.09 us
  transfers between devices with their start and end apart: 1, of which 1 were waited for; matrix products, arithmetic and copies ran while one was open for 0% of the time, Pallas kernels for 4%

profile of v8, /device:TPU:0, one launch (start us, length us, event | category | flops | bytes accessed | tf_op | source)
XLA Modules:
  0.0 40.8 jit_solution(14148026890061330549)
XLA Ops:
  0.6 1.3 %broadcast_in_dim.2 = s32[32,2,128]{2,1,0:T(2,128)} broadcast(s32[2,128]{1,0:T(2,128)} %bitcast.13), dimensions={1,2} | broadcast | bytes 33792 | tf_op jit(solution)/shard_map/broadcast_in_dim | solution.py:254
  1.9 7.3 %all-to-all-start = ((s32[32,2,128]{2,1,0:T(2,128)}), s32[32,2,128]{2,1,0:T(2,128)S(1)}, u32[]{:S(2)}, u32[]{:S(2)}) async-start(s32[32,2,128]{2,1,0:T(2,128)} %broadcast_in_dim.2), calls=%async_computation | async-start | bytes 65536 | tf_op jit(solution)/shard_map/all_to_all | solution.py:248
  9.2 1.5 %shard_map.93 = (bf16[512,128]{1,0:T(8,128)(2,1)S(1)}, s32[1,256]{1,0:T(1,128)S(1)}, bf16[256,320]{1,0:T(8,128)(2,1)S(1)}, bf16[160,512]{1,0:T(8,128)(2,1)S(1)},...) custom-call(s32[2,128]{1,0:T(2,128)} %bitcast.14, ...), custom_call_target="tpu_custom_call" | custom-call | flops 4000000000 | tf_op jit(solution)/shard_map/pallas_call | solution.py:255
  10.7 5.7 %all-to-all-done.asked_ref = s32[32,2,128]{2,1,0:T(2,128)S(1)} async-done(((s32[32,2,128]{2,1,0:T(2,128)}), s32[32,2,128]{2,1,0:T(2,128)S(1)}, u32[]{:S(2)}, u32[]{:S(2)}) %all-to-all-start) | async-done | bytes 32800 | tf_op jit(solution)/shard_map/all_to_all | solution.py:248
  16.4 0.0 copy-start
  16.4 0.0 copy-start.1
  16.4 0.7 %shard_map.94 = (bf16[320,128]{1,0:T(8,128)(2,1)S(1)}, bf16[320,512]{1,0:T(8,128)(2,1)S(1)}) custom-call(s32[32,2,128]{2,1,0:T(2,128)S(1)} %all-to-all-done.asked_ref, bf16[512,128]{1,0:T(8,128)(2,1)S(1)} %get-tuple-element.21.pull_ref), custom_call_target="tpu_custom_call" | custom-call | flops 8000000000 | tf_op jit(solution)/shard_map/pallas_call | solution.py:268
  17.2 9.5 %all_to_all.15 = bf16[32,5,2,128]{3,2,1,0:T(2,128)(2,1)S(1)} all-to-all(bf16[32,5,2,128]{3,2,1,0:T(2,128)(2,1)S(1)} %bitcast.12), channel_id=1, replica_groups=mesh['rep'=2,'shard'=16] {'rep','shard'}, dimensions={0} | all-to-all | bytes 163840 | tf_op jit(solution)/shard_map/all_to_all | solution.py:248
  26.6 0.0 copy-done
  26.6 0.0 copy-done.1
  26.6 3.9 %shard_map.95 = (f32[8,128]{1,0:T(8,128)}, bf16[320,128]{1,0:T(8,128)(2,1)S(1)}, bf16[320,512]{1,0:T(8,128)(2,1)S(1)}) custom-call(s32[1,256]{1,0:T(1,128)S(1)} %get-tuple-element.20.order_vmem, bf16[320,128]{1,0:T(8,128)(2,1)S(1)} %bitcast.9, bf16[256,320]{1,0:T(8,128)(2,1)S(1)} %get-tuple-element.23.take_ref, ...), custom_call_target="tpu_custom_call" | custom-call | tf_op jit(solution)/shard_map/pallas_call | solution.py:274
  30.6 9.2 %all_to_all.16 = bf16[32,5,2,128]{3,2,1,0:T(2,128)(2,1)S(1)} all-to-all(bf16[32,5,2,128]{3,2,1,0:T(2,128)(2,1)S(1)} %bitcast.11), channel_id=1, replica_groups=mesh['rep'=2,'shard'=16] {'rep','shard'}, dimensions={0} | all-to-all | bytes 163840 | tf_op jit(solution)/shard_map/all_to_all | solution.py:248
  39.7 1.1 %shard_map.96 = (f32[64,512]{1,0:T(8,128)}, f32[64,512]{1,0:T(8,128)}, f32[64,512]{1,0:T(8,128)}) custom-call(bf16[320,128]{1,0:T(8,128)(2,1)S(1)} %bitcast.10, bf16[320,512]{1,0:T(8,128)(2,1)S(1)} %get-tuple-element.27.mine_ref, bf16[320,512]{1,0:T(8,128)(2,1)S(1)} %get-tuple-element.28.other_ref, f32[64,512]{1,0:T(8,128)S(1)} %get-tuple-element.29.zt_ref, ...), custom_call_target="tpu_custom_call" | custom-call | tf_op jit(solution)/shard_map/pallas_call | solution.py:292
Async XLA Ops:
  1.9 14.5 %all-to-all-start = ((s32[32,2,128]{2,1,0:T(2,128)}), s32[32,2,128]{2,1,0:T(2,128)S(1)}, u32[]{:S(2)}, u32[]{:S(2)}) async-start(s32[32,2,128]{2,1,0:T(2,128)} %broadcast_in_dim.2), calls=%async_computation | async-start | bytes 65536 | tf_op jit(solution)/shard_map/all_to_all | solution.py:248
  16.4 10.2 %copy-start = (bf16[256,128,128]{2,1,0:T(8,128)(2,1)S(1)}, bf16[256,128,128]{2,1,0:T(8,128)(2,1)}, u32[]{:S(2)}) copy-start(bf16[256,128,128]{2,1,0:T(8,128)(2,1)} %tile_ref.1) | copy-start | bytes 25165828
  16.4 10.2 %copy-start.1 = (s32[8,128]{1,0:T(8,128)S(1)}, s32[8,128]{1,0:T(8,128)}, u32[]{:S(2)}) copy-start(s32[8,128]{1,0:T(8,128)} %labels_ref.1) | copy-start | bytes 12292
